TPU v7x, 32 devices: a whole 2x2x4 slice. The times are simulated.
32 devices in a mesh: row: 8 (over y, x, core), col: 4 (over z).
Axes of the slice: x: 2, y: 2, z: 4, core: 2. Of those that a mesh axis runs over, the one named last changes fastest.
Arguments:
- image: bfloat16 [384, 256, 256], P('row', 'col'), may hold values from -6 to 6
- norm_gain: float32 [2, 2, 256], replicated, may hold values from 0.1 to 1.9
- conv_first: bfloat16 [2, 3, 3, 256, 256], replicated, may hold values from -0.125 to 0.125
- conv_second: bfloat16 [2, 3, 3, 256, 256], replicated, may hold values from -0.125 to 0.125
- proj_in: bfloat16 [2, 256, 512], replicated, may hold values from -0.375 to 0.375
- block_mix: bfloat16 [2, 256, 256], replicated, may hold values from -0.375 to 0.375
- block_bias: float32 [2, 256], replicated, may hold values from 0.5 to 1.5
- grid_mix: bfloat16 [2, 32, 32], replicated, may hold values from -1 to 1
- grid_bias: float32 [2, 32], replicated, may hold values from 0.5 to 1.5
- proj_out: bfloat16 [2, 256, 256], replicated, may hold values from -0.375 to 0.375
Outputs:
- restored: bfloat16 [384, 256, 256], P('row', 'col')
All inputs are finite; a program needn't handle non-finite values.
Results may differ from a plain program's by a relative error of at most 0.012.
Values may be sent and summed in bfloat16 or wider, within the bound.
No kernel may reach another device: no remote copies, remote signals or barrier semaphores. Data moves between devices by JAX's collectives and lax.ppermute only.
A program may use at most 128 MiB of HBM per device.

v0:
```python
import functools
import math

import jax
import jax.numpy as jnp
from jax import lax
from jax.experimental import pallas as pl
from jax.experimental.pallas import tpu as pltpu
from jax.sharding import PartitionSpec as P

BLOCK = 16
LAYERS = 2
RIM = 2
GROUP_ONE = 10
GROUP_TWO = 8
MIB = 1 << 20

epsilon = 1e-06
ROOT = math.sqrt(2.0 / math.pi)

VMEM = pl.BlockSpec(memory_space=pltpu.VMEM)
ANY = pl.BlockSpec(memory_space=pltpu.HBM)


def parity(axis):
    return lax.rem(lax.axis_index(axis), 2)


def edge_factors():
    factors = []
    for axis in ("row", "col"):
        place = lax.axis_index(axis)
        for end in (0, lax.axis_size(axis) - 1):
            factors.append(jnp.where(place == end, 0.0, 1.0))
    return factors


def gelu(v):
    return 0.5 * v * (1.0 + jnp.tanh(ROOT * (v + 0.044715 * (v * v * v))))


def normalised(values, gain_row):
    average = jnp.mean(values, axis=-1, keepdims=True)
    centred = values - average
    variance = jnp.mean(centred * centred, axis=-1, keepdims=True)
    return centred * lax.rsqrt(variance + epsilon) * gain_row


def rounded(values):
    return values.astype(jnp.bfloat16).astype(jnp.float32)


def largest_divisor(total, most):
    return max(d for d in range(1, most + 1) if total % d == 0)


def spread(row, left_row, right_row, dst_ref, i, cols):
    channels = row.shape[-1]
    place = lax.broadcasted_iota(jnp.int32, row.shape, 0)
    before = jnp.where(place == 0, left_row, pltpu.roll(row, 1, 0))
    after = jnp.where(place == cols - 1, right_row, pltpu.roll(row, cols - 1, 0))
    dst_ref[i, :, 0:channels] = before.astype(jnp.bfloat16)
    dst_ref[i, :, channels : 2 * channels] = row.astype(jnp.bfloat16)
    dst_ref[i, :, 2 * channels : 3 * channels] = after.astype(jnp.bfloat16)


def pipelined(count, multiply, finish, slots):
    multiply(0, slots[0])
    pairs = (count - 1) // 2

    @pl.loop(0, pairs)
    def _(k):
        for u in range(2):
            multiply(2 * k + u + 1, slots[(u + 1) % 2])
            finish(2 * k + u, slots[u])

    if count % 2 == 0:
        multiply(count - 1, slots[1])
        finish(count - 2, slots[0])
    finish(count - 1, slots[(count - 1) % 2])


def in_hbm(values):
    return pltpu.with_memory_space_constraint(values, pltpu.HBM)


def front_kernel(
    layer,
    cur_ref,
    near_rows,
    far_rows,
    near_cols,
    far_cols,
    gain_ref,
    first_hbm,
    second_hbm,
    in_proj_hbm,
    mixed_ref,
    lu_ref,
    lv_ref,
    gu_ref,
    gv_ref,
    one_ref,
    two_ref,
    sides_ref,
    left_side,
    right_side,
    left_one,
    right_one,
    slot_a,
    slot_b,
    slot_c,
    slot_d,
    first_ref,
    second_ref,
    in_ref,
    sems,
):
    rows, cols, channels = cur_ref.shape
    feed = [
        pltpu.make_async_copy(src.at[layer], dst, sems.at[k])
        for k, (src, dst) in enumerate(
            ((first_hbm, first_ref), (second_hbm, second_ref), (in_proj_hbm, in_ref))
        )
    ]
    for copy in feed:
        copy.start()
    half = channels // 2
    near_top = parity("row") == 1
    near_left = parity("col") == 1
    edge_ref = edge_factors()
    gain_one = gain_ref[layer, 0:1, :]
    gain_two = gain_ref[layer, 1:2, :]
    long = rows + 2 * RIM

    spot = lax.broadcasted_iota(jnp.int32, (long, channels), 0)
    within = jnp.where(spot < RIM, edge_ref[0], jnp.where(spot < long - RIM, 1.0, edge_ref[1]))

    def chosen(near_low, side, near, far):
        low, high = (near, far) if side == 0 else (far, near)
        return jnp.where(near_low, low.astype(jnp.float32), high.astype(jnp.float32))

    for side in range(2):
        for c in range(RIM):
            sides_ref[side * RIM + c, 0:long] = rounded(
                normalised(chosen(near_left, side, near_cols[c], far_cols[c]), gain_one)
            ) * (within * edge_ref[2 + side])
    left_side[0:long, 0:channels] = sides_ref[0, 0:long]
    left_side[0:long, channels : 2 * channels] = sides_ref[1, 0:long]
    right_side[0:long, channels : 2 * channels] = sides_ref[2, 0:long]
    right_side[0:long, 2 * channels : 3 * channels] = sides_ref[3, 0:long]

    def norm_row(values, dst, keep=None):
        row = rounded(normalised(values, gain_one))
        if keep is not None:
            row = row * keep
        spread(row, sides_ref[1, pl.ds(dst, 1)], sides_ref[2, pl.ds(dst, 1)], one_ref, dst, cols)
        left_side[pl.ds(dst, 1), 2 * channels : 3 * channels] = row[0:1]
        right_side[pl.ds(dst, 1), 0:channels] = row[cols - 1 : cols]

    for r in range(RIM):
        norm_row(chosen(near_top, 0, near_rows[r], far_rows[r]), r, edge_ref[0])
        norm_row(chosen(near_top, 1, near_rows[r], far_rows[r]), RIM + rows + r, edge_ref[1])

    unroll = largest_divisor(rows, 4)

    @pl.loop(0, rows // unroll)
    def _(step):
        for u in range(unroll):
            i = step * unroll + u
            norm_row(cur_ref[i].astype(jnp.float32), i + RIM)

    feed[0].wait()

    def windows(src_ref, base, count):
        return jnp.concatenate(
            [
                src_ref[pl.ds(base + a, count)].reshape(count * cols, 3 * channels)
                for a in range(3)
            ],
            axis=1,
        )

    tall = rows + 2
    padded = left_one.shape[0]
    place = lax.broadcasted_iota(jnp.int32, (padded, channels), 0)
    inside = jnp.where(place == 0, edge_ref[0], 1.0)
    inside = jnp.where(place == tall - 1, edge_ref[1], inside)
    group = slot_a.shape[0] // cols

    def first_multiply(g, slot):
        window = windows(one_ref, g * group, group)
        if isinstance(g, int) and g == 0:
            sides = [
                jnp.concatenate([side[a : a + padded] for a in range(3)], axis=1)
                for side in (left_side, right_side)
            ]
            window = jnp.concatenate([window] + [v.astype(jnp.bfloat16) for v in sides], axis=0)
        total = jnp.dot(window, first_ref[...], preferred_element_type=jnp.float32)
        slot[...] = total[: group * cols]
        if isinstance(g, int) and g == 0:
            for k, one_side in enumerate((left_one, right_one)):
                start = group * cols + k * padded
                one_side[...] = rounded(
                    gelu(total[start : start + padded]) * (inside * edge_ref[2 + k])
                )

    def first_finish(g, slot):
        for u in range(group):
            i = g * group + u
            keep = jnp.where(i == 0, edge_ref[0], jnp.where(i == tall - 1, edge_ref[1], 1.0))
            row = rounded(gelu(slot[u * cols : (u + 1) * cols])) * keep
            spread(row, left_one[pl.ds(i, 1)], right_one[pl.ds(i, 1)], two_ref, i, cols)

    pipelined(tall // group, first_multiply, first_finish, (slot_a, slot_b))

    feed[1].wait()
    feed[2].wait()
    many = slot_c.shape[0] // cols

    def second_multiply(g, slot):
        slot[...] = jnp.dot(
            windows(two_ref, g * many, many),
            second_ref[...],
            preferred_element_type=jnp.float32,
        )

    def second_finish(g, slot):
        where = pl.ds(pl.multiple_of(g * many * cols, many * cols), many * cols)
        total = slot[...] + cur_ref[pl.ds(g * many, many)].reshape(
            many * cols, channels
        ).astype(jnp.float32)
        mixed_ref[where] = total
        normed = normalised(total, gain_two).astype(jnp.bfloat16)
        expanded = gelu(
            jnp.dot(normed, in_ref[...], preferred_element_type=jnp.float32)
        ).astype(jnp.bfloat16)
        for k, out in enumerate((lu_ref, lv_ref, gu_ref, gv_ref)):
            out[where] = expanded[:, k * half : (k + 1) * half]

    pipelined(rows // many, second_multiply, second_finish, (slot_c, slot_d))

def front(layer, cur, rim_rows, rim_cols, gains, first, second, proj):
    rows, cols, channels = cur.shape
    pixels = rows * cols
    half = channels // 2
    long = rows + 2 * RIM
    padded = -(-(rows + 2) // 16) * 16
    tall = padded + 8
    group = largest_divisor(rows + 2, GROUP_ONE)
    many = largest_divisor(rows, GROUP_TWO)
    bf = jnp.bfloat16
    f32 = jnp.float32
    outs = [jax.ShapeDtypeStruct((pixels, channels), f32)]
    outs += [jax.ShapeDtypeStruct((pixels, half), bf)] * 4
    return pl.pallas_call(
        functools.partial(front_kernel, layer),
        out_shape=outs,
        in_specs=[VMEM] * 6 + [ANY] * 3,
        out_specs=[VMEM] * 5,
        scratch_shapes=[
            pltpu.VMEM((long, cols, 3 * channels), bf),
            pltpu.VMEM((rows + 2, cols, 3 * channels), bf),
            pltpu.VMEM((2 * RIM, tall, channels), f32),
            pltpu.VMEM((tall, 3 * channels), f32),
            pltpu.VMEM((tall, 3 * channels), f32),
            pltpu.VMEM((padded, channels), f32),
            pltpu.VMEM((padded, channels), f32),
            pltpu.VMEM((group * cols, channels), f32),
            pltpu.VMEM((group * cols, channels), f32),
            pltpu.VMEM((many * cols, channels), f32),
            pltpu.VMEM((many * cols, channels), f32),
            pltpu.VMEM(first.shape[1:], bf),
            pltpu.VMEM(second.shape[1:], bf),
            pltpu.VMEM(proj.shape[1:], bf),
            pltpu.SemaphoreType.DMA((3,)),
        ],
        compiler_params=pltpu.CompilerParams(vmem_limit_bytes=34 * MIB),
        cost_estimate=pl.CostEstimate(
            flops=2 * pixels * channels * channels * 20,
            bytes_accessed=12 << 20,
            transcendentals=3 * pixels * channels,
        ),
        name="front",
    )(cur, *rim_rows, *rim_cols, gains, *(in_hbm(w) for w in (first, second, proj)))


def local_kernel(
    layer, lu_ref, lv_ref, mix_ref, bias_ref, grid_ref, grid_bias_ref, out_ref, tiles_ref, shift_ref
):
    rows, cols, half = lu_ref.shape
    down, across = rows // BLOCK, cols // BLOCK
    pair = 2 if across % 2 == 0 else 1
    area = BLOCK * BLOCK
    spot = lax.broadcasted_iota(jnp.int32, (area, area), 0)
    same = spot == lax.broadcasted_iota(jnp.int32, (area, area), 1)
    bias = jnp.sum(jnp.where(same, bias_ref[layer : layer + 1], 0.0), axis=1, keepdims=True)
    for i in range(down):
        r = slice(i * BLOCK, (i + 1) * BLOCK)
        for j in range(0, across, pair):
            cut = [slice((j + k) * BLOCK, (j + k + 1) * BLOCK) for k in range(pair)]
            v = jnp.concatenate(
                [lv_ref[r, c].reshape(BLOCK * BLOCK, half) for c in cut], axis=1
            )
            m = jnp.dot(mix_ref[layer], v, preferred_element_type=jnp.float32) + bias
            for k, c in enumerate(cut):
                u = lu_ref[r, c].reshape(BLOCK * BLOCK, half).astype(jnp.float32)
                gated = (u * m[:, k * half : (k + 1) * half]).astype(jnp.bfloat16)
                out_ref[r, c] = gated.reshape(BLOCK, BLOCK, half)
    cells = grid_ref.shape[-1]
    wide = tiles_ref.shape[0]
    tile = wide // cells
    down_of = lax.broadcasted_iota(jnp.int32, (wide, cells), 0) // tile
    chosen = down_of == lax.broadcasted_iota(jnp.int32, (wide, cells), 1)
    shift = jnp.sum(jnp.where(chosen, grid_bias_ref[layer : layer + 1], 0.0), axis=1, keepdims=True)
    shift_ref[...] = jnp.broadcast_to(shift, shift_ref.shape)
    pick = chosen.astype(jnp.bfloat16)
    across_of = lax.broadcasted_iota(jnp.int32, (cells, wide), 1) // tile
    lay = (across_of == lax.broadcasted_iota(jnp.int32, (cells, wide), 0)).astype(jnp.bfloat16)
    tall = jnp.dot(pick, grid_ref[layer], preferred_element_type=jnp.float32)
    full = jnp.dot(tall.astype(jnp.bfloat16), lay, preferred_element_type=jnp.float32)
    p = lax.broadcasted_iota(jnp.int32, (wide, wide), 0) % tile
    q = lax.broadcasted_iota(jnp.int32, (wide, wide), 1) % tile
    tiles_ref[...] = jnp.where(p == q, full, 0.0).astype(jnp.bfloat16)


def local(layer, lu, lv, mix, bias, grid, grid_bias, tile):
    rows, cols, half = lu.shape
    wide = grid.shape[-1] * tile
    return pl.pallas_call(
        functools.partial(local_kernel, layer),
        out_shape=[
            jax.ShapeDtypeStruct(lu.shape, jnp.bfloat16),
            jax.ShapeDtypeStruct((wide, wide), jnp.bfloat16),
            jax.ShapeDtypeStruct((wide, half), jnp.float32),
        ],
        in_specs=[VMEM] * 6,
        out_specs=[VMEM] * 3,
        compiler_params=pltpu.CompilerParams(vmem_limit_bytes=12 * MIB),
        cost_estimate=pl.CostEstimate(
            flops=2 * rows * cols * half * BLOCK * BLOCK,
            bytes_accessed=6 * rows * cols * half,
            transcendentals=0,
        ),
        name="local",
    )(lu, lv, mix, bias, grid, grid_bias)


def grid_kernel(got_ref, mix_ref, bias_ref, out_ref):
    cells, share, half = got_ref.shape
    tile = mix_ref.shape[0] // cells
    step = 2 * tile if share % (2 * tile) == 0 else tile
    for k in range(share // step):
        parts = [slice(t, t + tile) for t in range(k * step, (k + 1) * step, tile)]
        if tile == 16:
            v = [got_ref[:, part].reshape(cells * tile, half) for part in parts]
        else:
            v = [
                got_ref[:, part].astype(jnp.float32).reshape(cells * tile, half).astype(jnp.bfloat16)
                for part in parts
            ]
        m = jnp.dot(
            mix_ref[...], jnp.concatenate(v, axis=1), preferred_element_type=jnp.float32
        )
        for n, part in enumerate(parts):
            blend = m[:, n * half : (n + 1) * half] + bias_ref[...]
            if tile == 16:
                out_ref[:, part] = blend.astype(jnp.bfloat16).reshape(cells, tile, half)
            else:
                out_ref[:, part] = blend.reshape(cells, tile, half).astype(jnp.bfloat16)

def grid_mixing(got, mix, bias):
    cells, share, half = got.shape
    return pl.pallas_call(
        grid_kernel,
        out_shape=jax.ShapeDtypeStruct(got.shape, jnp.bfloat16),
        in_specs=[VMEM] * 3,
        out_specs=VMEM,
        compiler_params=pltpu.CompilerParams(vmem_limit_bytes=10 * MIB),
        name="grid_mixing",
    )(got, mix, bias)


def keep_strips(top, bottom, strip_ref, near_ref, far_ref, left_ref, right_ref):
    odd_row = parity("row")

    @pl.when(odd_row == 0)
    def _():
        near_ref[...] = bottom
        far_ref[...] = top

    @pl.when(odd_row == 1)
    def _():
        near_ref[...] = top
        far_ref[...] = bottom

    left_ref[...] = strip_ref[0].astype(jnp.bfloat16)
    right_ref[...] = strip_ref[1].astype(jnp.bfloat16)


def back_kernel(layer, last, mixed_ref, gl_ref, gu_ref, gm_ref, proj_ref, cur_ref, *refs):
    rows, cols, channels = cur_ref.shape
    many = largest_divisor(rows, 8)

    @pl.loop(0, rows // many)
    def _(g):
        where = pl.ds(pl.multiple_of(g * many * cols, many * cols), many * cols)
        gated = gu_ref[where].astype(jnp.float32) * gm_ref[where].astype(jnp.float32)
        joined = jnp.concatenate([gl_ref[where], gated.astype(jnp.bfloat16)], axis=1)
        total = mixed_ref[where] + jnp.dot(
            joined, proj_ref[layer], preferred_element_type=jnp.float32
        )
        cur_ref[pl.ds(g * many, many)] = total.reshape(many, cols, channels).astype(jnp.bfloat16)
        if not last:
            strip_ref = refs[-1]
            for u in range(many):
                for c in range(RIM):
                    low = u * cols + c
                    high = (u + 1) * cols - RIM + c
                    strip_ref[0, c, pl.ds(g * many + u, 1)] = total[low : low + 1]
                    strip_ref[1, c, pl.ds(g * many + u, 1)] = total[high : high + 1]

    if not last:
        *strip_refs, strip_ref = refs
        keep_strips(cur_ref[0:RIM], cur_ref[rows - RIM : rows], strip_ref, *strip_refs)


def strip_shapes(shape):
    rows, cols, channels = shape
    return [jax.ShapeDtypeStruct((RIM, cols, channels), jnp.bfloat16)] * 2 + [
        jax.ShapeDtypeStruct((RIM, rows, channels), jnp.bfloat16)
    ] * 2


def back(layer, last, mixed, gl, gu, gm, proj, shape):
    rows, cols, channels = shape
    f32 = jnp.float32
    outs = [jax.ShapeDtypeStruct(shape, jnp.bfloat16)]
    scratch = []
    if not last:
        outs += strip_shapes(shape)
        scratch.append(pltpu.VMEM((2, RIM, rows, channels), f32))
    return pl.pallas_call(
        functools.partial(back_kernel, layer, last),
        out_shape=outs,
        in_specs=[VMEM] * 5,
        out_specs=[VMEM] * len(outs),
        scratch_shapes=scratch,
        compiler_params=pltpu.CompilerParams(vmem_limit_bytes=16 * MIB),
        cost_estimate=pl.CostEstimate(
            flops=2 * rows * cols * channels * channels,
            bytes_accessed=rows * cols * channels * 9,
            transcendentals=0,
        ),
        name="back",
    )(mixed, gl, gu, gm, proj)


def strips_kernel(image_hbm, cur_ref, *refs):
    *strip_refs, strip_ref, sem = refs
    rows, cols, channels = image_hbm.shape
    copy = pltpu.make_async_copy(image_hbm, cur_ref, sem.at[0])
    copy.start()
    copy.wait()
    side = math.gcd(cols, 16)
    for i in range(rows):
        low = cur_ref[i, 0:side].astype(jnp.float32)
        high = cur_ref[i, cols - side : cols].astype(jnp.float32)
        for c in range(RIM):
            strip_ref[0, c, i : i + 1] = low[c : c + 1]
            strip_ref[1, c, i : i + 1] = high[side - RIM + c : side - RIM + c + 1]
    keep_strips(cur_ref[0:RIM], cur_ref[rows - RIM : rows], strip_ref, *strip_refs)


def strips(image):
    rows, cols, channels = image.shape
    return pl.pallas_call(
        strips_kernel,
        out_shape=[jax.ShapeDtypeStruct(image.shape, jnp.bfloat16)] + strip_shapes(image.shape),
        in_specs=[ANY],
        out_specs=[VMEM] * 5,
        scratch_shapes=[
            pltpu.VMEM((2, RIM, rows, channels), jnp.float32),
            pltpu.SemaphoreType.DMA((1,)),
        ],
        compiler_params=pltpu.CompilerParams(vmem_limit_bytes=8 * MIB),
        name="strips",
    )(in_hbm(image))


def traded(axis, near, far):
    count = lax.axis_size(axis)
    inner = [(i, i ^ 1) for i in range(count)]
    outer = [(i, (i + 1) % count) for i in range(1, count, 2)]
    outer += [(target, source) for source, target in outer]
    far = lax.ppermute(far, axis, outer)
    near = lax.ppermute(near, axis, inner)
    return near, far


def columns_kernel(near_rows, far_rows, left_ref, right_ref, near_ref, far_ref):
    odd_row, odd_col = parity("row"), parity("col")
    rim, rows, _ = left_ref.shape
    cols = near_rows.shape[1]
    near_top = odd_row == 1
    for side, own_ref in ((0, left_ref), (1, right_ref)):
        wanted = (odd_col == 1) if side == 0 else (odd_col == 0)
        first = 0 if side == 0 else cols - rim

        def ends(rows_ref, c):
            return [rows_ref[r, first + c : first + c + 1].astype(jnp.float32) for r in range(rim)]

        strips = []
        for c in range(rim):
            close, other = ends(near_rows, c), ends(far_rows, c)
            top = [jnp.where(near_top, x, y) for x, y in zip(close, other)]
            bottom = [jnp.where(near_top, y, x) for x, y in zip(close, other)]
            strips.append(
                jnp.concatenate(top + [own_ref[c].astype(jnp.float32)] + bottom, axis=0).astype(
                    jnp.bfloat16
                )
            )

        @pl.when(wanted)
        def _():
            for c in range(rim):
                near_ref[c] = strips[c]

        @pl.when(jnp.logical_not(wanted))
        def _():
            for c in range(rim):
                far_ref[c] = strips[c]


def columns(near_rows, far_rows, left, right):
    rim, rows, channels = left.shape
    return pl.pallas_call(
        columns_kernel,
        out_shape=[jax.ShapeDtypeStruct((rim, rows + 2 * rim, channels), jnp.bfloat16)] * 2,
        in_specs=[VMEM] * 4,
        out_specs=[VMEM] * 2,
        compiler_params=pltpu.CompilerParams(vmem_limit_bytes=8 * MIB),
        name="columns",
    )(near_rows, far_rows, left, right)


def rims(near_rows, far_rows, left, right):
    rim_rows = traded("row", near_rows, far_rows)
    return rim_rows, traded("col", *columns(*rim_rows, left, right))


def on_device(
    image,
    norm_gain,
    conv_first,
    conv_second,
    proj_in,
    block_mix,
    block_bias,
    grid_mix,
    grid_bias,
    proj_out,
):
    rows, cols, channels = image.shape
    half = channels // 2
    row_count = lax.axis_size("row")
    col_count = lax.axis_size("col")
    cells = row_count * col_count
    pixels = rows * cols
    share = pixels // cells
    tile = math.gcd(share, 16)
    first = conv_first.reshape(LAYERS, 9 * channels, channels)
    second = conv_second.reshape(LAYERS, 9 * channels, channels)
    current, *own = strips(image)
    for layer in range(LAYERS):
        last = layer == LAYERS - 1
        rim_rows, rim_cols = rims(*own)
        mixed, lu, lv, gu, gv = front(
            layer, current, rim_rows, rim_cols, norm_gain, first, second, proj_in
        )
        gl, mix_tiles, bias_tiles = local(
            layer,
            lu.reshape(rows, cols, half),
            lv.reshape(rows, cols, half),
            block_mix,
            block_bias,
            grid_mix,
            grid_bias,
            tile,
        )
        gv, gl = lax.optimization_barrier((gv, gl))
        got = lax.all_to_all(
            gv.reshape(1, cells, share, half), ("row", "col"), 1, 0, tiled=True
        )
        blend = grid_mixing(got.reshape(cells, share, half), mix_tiles, bias_tiles)
        gm = lax.all_to_all(
            blend.reshape(cells, 1, share, half), ("row", "col"), 0, 1, tiled=True
        )
        current, *own = back(
            layer,
            last,
            mixed,
            gl.reshape(pixels, half),
            gu,
            gm.reshape(pixels, half),
            proj_out,
            image.shape,
        )
    return current


def solution(mesh):
    placed = (P("row", "col", None), P(), P(), P(), P(), P(), P(), P(), P(), P())
    return jax.shard_map(
        on_device, mesh=mesh, in_specs=placed, out_specs=P("row", "col", None), check_vma=False
    )
```

profile of v0, /device:TPU:1, one launch (start us, length us, event | category | flops | bytes accessed | tf_op | source)
XLA Modules:
  0.0 162.6 jit_solution(13027645208228397847)
XLA Ops:
  0.0 1.5 strips.1
  1.6 0.1 collective-permute-start
  1.6 2.6 %collective-permute-start.1 = (bf16[2,64,256]{2,1,0:T(8,128)(2,1)S(1)}, bf16[2,64,256]{2,1,0:T(8,128)(2,1)S(1)}, u32[]{:S(2)}, u32[]{:S(2)}) collective-permute-start(bf16[2,64,256]{2,1,0:T(8,128)(2,1)S(1)} %get-tuple-element.41), channel_id=1, source_target_pairs={{4,8},{12,16},{20,24},{28,0},{8,4},{16,12},{24,20},{0,28},{5,9},{1... | collective-permute-start | bytes 196616 | tf_op jit(solution)/shard_map/ppermute | solution.py:496
  4.3 0.0 collective-permute-done.near_rows
  4.3 2.2 %collective-permute-done.1.far_rows = bf16[2,64,256]{2,1,0:T(8,128)(2,1)S(1)} collective-permute-done((bf16[2,64,256]{2,1,0:T(8,128)(2,1)S(1)}, bf16[2,64,256]{2,1,0:T(8,128)(2,1)S(1)}, u32[]{:S(2)}, u32[]{:S(2)}) %collective-permute-start.1) | collective-permute-done | bytes 65568 | tf_op jit(solution)/shard_map/ppermute | solution.py:496
  6.6 2.2 %collective-permute-start.2 = (bf16[2,52,256]{2,1,0:T(8,128)(2,1)S(1)}, bf16[2,52,256]{2,1,0:T(8,128)(2,1)S(1)}, u32[]{:S(2)}, u32[]{:S(2)}) collective-permute-start(bf16[2,52,256]{2,1,0:T(8,128)(2,1)S(1)} %get-tuple-element.44), channel_id=1, source_target_pairs={{0,1},{1,0},{2,3},{3,2},{4,5},{5,4},{6,7},{7,6},{8,9},{9,8},{10,11... | collective-permute-start | bytes 159752 | tf_op jit(solution)/shard_map/ppermute | solution.py:497
  8.8 2.2 %collective-permute-start.3 = (bf16[2,52,256]{2,1,0:T(8,128)(2,1)S(1)}, bf16[2,52,256]{2,1,0:T(8,128)(2,1)S(1)}, u32[]{:S(2)}, u32[]{:S(2)}) collective-permute-start(bf16[2,52,256]{2,1,0:T(8,128)(2,1)S(1)} %get-tuple-element.45), channel_id=1, source_target_pairs={{1,2},{3,0},{2,1},{0,3},{5,6},{7,4},{6,5},{4,7},{9,10},{11,8},{10,... | collective-permute-start | bytes 159752 | tf_op jit(solution)/shard_map/ppermute | solution.py:496
  11.0 0.0 collective-permute-done.2.near_cols
  11.0 3.1 %collective-permute-done.3.far_cols = bf16[2,52,256]{2,1,0:T(8,128)(2,1)S(1)} collective-permute-done((bf16[2,52,256]{2,1,0:T(8,128)(2,1)S(1)}, bf16[2,52,256]{2,1,0:T(8,128)(2,1)S(1)}, u32[]{:S(2)}, u32[]{:S(2)}) %collective-permute-start.3) | collective-permute-done | bytes 53280 | tf_op jit(solution)/shard_map/ppermute | solution.py:496
  14.2 0.0 copy-start.5
  14.2 0.7 copy-done.5
  14.8 0.0 copy-start.1
  14.8 0.0 copy-start.2
  14.8 0.0 copy-start.3
  14.8 0.0 copy-start.4
  14.9 15.8 %front.2 = (f32[3072,256]{1,0:T(8,128)S(1)}, bf16[3072,128]{1,0:T(8,128)(2,1)S(1)}, bf16[3072,128]{1,0:T(8,128)(2,1)S(1)}, bf16[3072,128]{1,0:T(8,128)(2,1)S(1)}, bf16[3072,128]{1,0:T(8,128)(2,1)S(1)}) custom-call(bf16[48,64,256]{2,1,0:T(8,128)(2,1)S(1)} %get-tuple-element.39.cur_ref, bf16[2,64,256]{2,1,0:T(8,128)(2,1)S(1)} %collective-permute-done.near_rows, ...), custom_call_target="tpu_custom_call" | custom-call | flops 8053063680 | bytes 12582912 | tf_op jit(solution)/shard_map/front/pallas_call | solution.py:256
  30.7 0.0 copy-done.1
  30.7 0.0 copy-done.2
  30.7 0.0 copy-done.3
  30.7 0.0 copy-done.4
  30.7 0.7 local.2
  31.4 26.3 %all_to_all.16 = bf16[1,32,96,128]{3,2,0,1:T(8,128)(2,1)S(1)} all-to-all(bf16[1,32,96,128]{3,2,0,1:T(8,128)(2,1)S(1)} %bitcast.31), channel_id=1, replica_groups=mesh['row'=8,'col'=4] {'row','col'}, dimensions={1} | all-to-all | bytes 1572864 | tf_op jit(solution)/shard_map/all_to_all | solution.py:592
  57.7 0.0 copy-start
  57.7 0.6 grid_mixing.2
  58.2 23.8 %all_to_all.17 = bf16[32,1,96,128]{3,2,1,0:T(8,128)(2,1)S(1)} all-to-all(bf16[32,1,96,128]{3,2,1,0:T(8,128)(2,1)S(1)} %bitcast.27), channel_id=1, replica_groups=mesh['row'=8,'col'=4] {'row','col'}, dimensions={0} | all-to-all | bytes 1572864 | tf_op jit(solution)/shard_map/all_to_all | solution.py:596
  82.0 0.0 copy-done
  82.0 0.0 copy-start.6
  82.0 1.5 back.2
  83.5 0.1 collective-permute-start.4
  83.6 1.6 collective-permute-start.5
  85.2 0.0 collective-permute-done.4.near_rows
  85.2 2.5 %collective-permute-done.5.far_rows = bf16[2,64,256]{2,1,0:T(8,128)(2,1)S(1)} collective-permute-done((bf16[2,64,256]{2,1,0:T(8,128)(2,1)S(1)}, bf16[2,64,256]{2,1,0:T(8,128)(2,1)S(1)}, u32[]{:S(2)}, u32[]{:S(2)}) %collective-permute-start.5) | collective-permute-done | bytes 65568 | tf_op jit(solution)/shard_map/ppermute | solution.py:496
  87.7 0.2 columns.3
  87.9 1.6 collective-permute-start.6
  89.5 0.8 collective-permute-start.7
  90.3 0.8 collective-permute-done.6.near_cols
  91.1 3.3 %collective-permute-done.7.far_cols = bf16[2,52,256]{2,1,0:T(8,128)(2,1)S(1)} collective-permute-done((bf16[2,52,256]{2,1,0:T(8,128)(2,1)S(1)}, bf16[2,52,256]{2,1,0:T(8,128)(2,1)S(1)}, u32[]{:S(2)}, u32[]{:S(2)}) %collective-permute-start.7) | collective-permute-done | bytes 53280 | tf_op jit(solution)/shard_map/ppermute | solution.py:496
  94.4 0.0 copy-done.6
  94.4 15.9 %front.3 = (f32[3072,256]{1,0:T(8,128)S(1)}, bf16[3072,128]{1,0:T(8,128)(2,1)S(1)}, bf16[3072,128]{1,0:T(8,128)(2,1)S(1)}, bf16[3072,128]{1,0:T(8,128)(2,1)S(1)}, bf16[3072,128]{1,0:T(8,128)(2,1)S(1)}) custom-call(bf16[48,64,256]{2,1,0:T(8,128)(2,1)S(1)} %get-tuple-element.56.cur_ref, bf16[2,64,256]{2,1,0:T(8,128)(2,1)S(1)} %collective-permute-done.4.near_rows, ...), custom_call_target="tpu_custom_call" | custom-call | flops 8053063680 | bytes 12582912 | tf_op jit(solution)/shard_map/front/pallas_call | solution.py:256
  110.3 0.7 local.3
  111.0 24.8 %all_to_all.18 = bf16[1,32,96,128]{3,2,0,1:T(8,128)(2,1)S(1)} all-to-all(bf16[1,32,96,128]{3,2,0,1:T(8,128)(2,1)S(1)} %bitcast.32), channel_id=1, replica_groups=mesh['row'=8,'col'=4] {'row','col'}, dimensions={1} | all-to-all | bytes 1572864 | tf_op jit(solution)/shard_map/all_to_all | solution.py:592
  135.7 0.6 grid_mixing.3
  136.3 23.8 %all_to_all.19 = bf16[32,1,96,128]{3,2,1,0:T(8,128)(2,1)S(1)} all-to-all(bf16[32,1,96,128]{3,2,1,0:T(8,128)(2,1)S(1)} %bitcast.28), channel_id=1, replica_groups=mesh['row'=8,'col'=4] {'row','col'}, dimensions={0} | all-to-all | bytes 1572864 | tf_op jit(solution)/shard_map/all_to_all | solution.py:596
  160.0 2.6 %back.3 = bf16[48,64,256]{2,1,0:T(8,128)(2,1)} custom-call(f32[3072,256]{1,0:T(8,128)S(1)} %get-tuple-element.63.mixed_ref, bf16[3072,128]{1,0:T(8,128)(2,1)S(1)} %bitcast.30, bf16[3072,128]{1,0:T(8,128)(2,1)S(1)} %get-tuple-element.69.gu_ref, bf16[3072,128]{1,0:T(8,128)(2,1)S(1)} %bitcast.24, bf16[2,256,256]{2,1,0:T(8,128)(2,1)S(1)} %copy-done), custom_call_target="tpu_custom_call" | custom-call | flops 402653184 | bytes 7077888 | tf_op jit(solution)/shard_map/back/pallas_call | solution.py:443
  (1 shorter events, 0.0 us)
Async XLA Ops:
  1.6 2.7 %collective-permute-start = (bf16[2,64,256]{2,1,0:T(8,128)(2,1)S(1)}, bf16[2,64,256]{2,1,0:T(8,128)(2,1)S(1)}, u32[]{:S(2)}, u32[]{:S(2)}) collective-permute-start(bf16[2,64,256]{2,1,0:T(8,128)(2,1)S(1)} %get-tuple-element.40), channel_id=1, source_target_pairs={{0,4},{4,0},{8,12},{12,8},{16,20},{20,16},{24,28},{28,24},{1,5},{5... | collective-permute-start | bytes 196616 | tf_op jit(solution)/shard_map/ppermute | solution.py:497
  1.6 4.9 %collective-permute-start.1 = (bf16[2,64,256]{2,1,0:T(8,128)(2,1)S(1)}, bf16[2,64,256]{2,1,0:T(8,128)(2,1)S(1)}, u32[]{:S(2)}, u32[]{:S(2)}) collective-permute-start(bf16[2,64,256]{2,1,0:T(8,128)(2,1)S(1)} %get-tuple-element.41), channel_id=1, source_target_pairs={{4,8},{12,16},{20,24},{28,0},{8,4},{16,12},{24,20},{0,28},{5,9},{1... | collective-permute-start | bytes 196616 | tf_op jit(solution)/shard_map/ppermute | solution.py:496
  6.6 4.4 %collective-permute-start.2 = (bf16[2,52,256]{2,1,0:T(8,128)(2,1)S(1)}, bf16[2,52,256]{2,1,0:T(8,128)(2,1)S(1)}, u32[]{:S(2)}, u32[]{:S(2)}) collective-permute-start(bf16[2,52,256]{2,1,0:T(8,128)(2,1)S(1)} %get-tuple-element.44), channel_id=1, source_target_pairs={{0,1},{1,0},{2,3},{3,2},{4,5},{5,4},{6,7},{7,6},{8,9},{9,8},{10,11... | collective-permute-start | bytes 159752 | tf_op jit(solution)/shard_map/ppermute | solution.py:497
  8.8 5.3 %collective-permute-start.3 = (bf16[2,52,256]{2,1,0:T(8,128)(2,1)S(1)}, bf16[2,52,256]{2,1,0:T(8,128)(2,1)S(1)}, u32[]{:S(2)}, u32[]{:S(2)}) collective-permute-start(bf16[2,52,256]{2,1,0:T(8,128)(2,1)S(1)} %get-tuple-element.45), channel_id=1, source_target_pairs={{1,2},{3,0},{2,1},{0,3},{5,6},{7,4},{6,5},{4,7},{9,10},{11,8},{10,... | collective-permute-start | bytes 159752 | tf_op jit(solution)/shard_map/ppermute | solution.py:496
  14.2 0.7 copy-start.5
  14.8 15.9 %copy-start.1 = (bf16[2,256,256]{2,1,0:T(8,128)(2,1)S(1)}, bf16[2,256,256]{2,1,0:T(8,128)(2,1)}, u32[]{:S(2)}) copy-start(bf16[2,256,256]{2,1,0:T(8,128)(2,1)} %mix_ref.3) | copy-start | bytes 786436
  14.8 15.9 %copy-start.2 = (bf16[2,32,32]{2,1,0:T(8,128)(2,1)S(1)}, bf16[2,32,32]{2,1,0:T(8,128)(2,1)}, u32[]{:S(2)}) copy-start(bf16[2,32,32]{2,1,0:T(8,128)(2,1)} %grid_ref.3) | copy-start | bytes 12292
  14.8 15.9 %copy-start.3 = (f32[2,256]{1,0:T(2,128)S(1)}, f32[2,256]{1,0:T(2,128)}, u32[]{:S(2)}) copy-start(f32[2,256]{1,0:T(2,128)} %bias_ref.3) | copy-start | bytes 6148
  14.8 15.9 %copy-start.4 = (f32[2,32]{1,0:T(2,128)S(1)}, f32[2,32]{1,0:T(2,128)}, u32[]{:S(2)}) copy-start(f32[2,32]{1,0:T(2,128)} %grid_bias_ref.3) | copy-start | bytes 772
  57.7 24.3 %copy-start = (bf16[2,256,256]{2,1,0:T(8,128)(2,1)S(1)}, bf16[2,256,256]{2,1,0:T(8,128)(2,1)}, u32[]{:S(2)}) copy-start(bf16[2,256,256]{2,1,0:T(8,128)(2,1)} %proj_ref.3) | copy-start | bytes 786436
  82.0 12.4 %copy-start.6 = (f32[2,2,256]{2,1,0:T(2,128)S(1)}, f32[2,2,256]{2,1,0:T(2,128)}, u32[]{:S(2)}) copy-start(f32[2,2,256]{2,1,0:T(2,128)} %gain_ref.3) | copy-start | bytes 12292
  83.5 1.7 %collective-permute-start.4 = (bf16[2,64,256]{2,1,0:T(8,128)(2,1)S(1)}, bf16[2,64,256]{2,1,0:T(8,128)(2,1)S(1)}, u32[]{:S(2)}, u32[]{:S(2)}) collective-permute-start(bf16[2,64,256]{2,1,0:T(8,128)(2,1)S(1)} %get-tuple-element.57), channel_id=1, source_target_pairs={{0,4},{4,0},{8,12},{12,8},{16,20},{20,16},{24,28},{28,24},{1,5},{5... | collective-permute-start | bytes 196616 | tf_op jit(solution)/shard_map/ppermute | solution.py:497
  83.6 4.1 %collective-permute-start.5 = (bf16[2,64,256]{2,1,0:T(8,128)(2,1)S(1)}, bf16[2,64,256]{2,1,0:T(8,128)(2,1)S(1)}, u32[]{:S(2)}, u32[]{:S(2)}) collective-permute-start(bf16[2,64,256]{2,1,0:T(8,128)(2,1)S(1)} %get-tuple-element.58), channel_id=1, source_target_pairs={{4,8},{12,16},{20,24},{28,0},{8,4},{16,12},{24,20},{0,28},{5,9},{1... | collective-permute-start | bytes 196616 | tf_op jit(solution)/shard_map/ppermute | solution.py:496
  87.9 3.2 %collective-permute-start.6 = (bf16[2,52,256]{2,1,0:T(8,128)(2,1)S(1)}, bf16[2,52,256]{2,1,0:T(8,128)(2,1)S(1)}, u32[]{:S(2)}, u32[]{:S(2)}) collective-permute-start(bf16[2,52,256]{2,1,0:T(8,128)(2,1)S(1)} %get-tuple-element.61), channel_id=1, source_target_pairs={{0,1},{1,0},{2,3},{3,2},{4,5},{5,4},{6,7},{7,6},{8,9},{9,8},{10,11... | collective-permute-start | bytes 159752 | tf_op jit(solution)/shard_map/ppermute | solution.py:497
  89.5 4.9 %collective-permute-start.7 = (bf16[2,52,256]{2,1,0:T(8,128)(2,1)S(1)}, bf16[2,52,256]{2,1,0:T(8,128)(2,1)S(1)}, u32[]{:S(2)}, u32[]{:S(2)}) collective-permute-start(bf16[2,52,256]{2,1,0:T(8,128)(2,1)S(1)} %get-tuple-element.62), channel_id=1, source_target_pairs={{1,2},{3,0},{2,1},{0,3},{5,6},{7,4},{6,5},{4,7},{9,10},{11,8},{10,... | collective-permute-start | bytes 159752 | tf_op jit(solution)/shard_map/ppermute | solution.py:496
where the time goes:
time: 163 us
  blocking collectives  98.5 us (60%)
  Pallas kernels  40 us (25%)
  waiting for transfers between devices  12 us (7%)
  starting transfers between devices  11.2 us (7%)
    all_to_all x2, blocking collectives, on_device(): lax.all_to_all(gv.reshape(1, cells, share, half), ('row', 'col'), 1, 0, t...  51 us
    all_to_all x2, blocking collectives, on_device(): lax.all_to_all(blend.reshape(cells, 1, share, half), ('row', 'col'), 0, 1...  47.5 us
    pallas_call x2, Pallas kernels, front(): pl.pallas_call(functools.partial(front_kernel, layer), out_shape=outs, in...  31.7 us
    ppermute x4, waiting for transfers between devices, traded(): far = lax.ppermute(far, axis, outer)  11.2 us
    ppermute x4, starting transfers between devices, traded(): far = lax.ppermute(far, axis, outer)  7.23 us
    pallas_call x2, Pallas kernels, back(): pl.pallas_call(functools.partial(back_kernel, layer, last), out_shape=out...  4.05 us
    ppermute x4, starting transfers between devices, traded(): near = lax.ppermute(near, axis, inner)  4 us
  transfers between devices with their start and end apart: 8, of which 5 were waited for; matrix products, arithmetic and copies ran while one was open for 0% of the time, Pallas kernels for 0%

commit v1 on v0

--- a/solution.py
+++ b/solution.py
@@ -8,11 +8,12 @@
 from jax.experimental.pallas import tpu as pltpu
 from jax.sharding import PartitionSpec as P
 
+
 BLOCK = 16
 LAYERS = 2
 RIM = 2
-GROUP_ONE = 10
-GROUP_TWO = 8
+GROUP_ONE = 5
+GROUP_TWO = 12
 MIB = 1 << 20
 
 epsilon = 1e-06
@@ -64,22 +65,6 @@
     dst_ref[i, :, 2 * channels : 3 * channels] = after.astype(jnp.bfloat16)
 
 
-def pipelined(count, multiply, finish, slots):
-    multiply(0, slots[0])
-    pairs = (count - 1) // 2
-
-    @pl.loop(0, pairs)
-    def _(k):
-        for u in range(2):
-            multiply(2 * k + u + 1, slots[(u + 1) % 2])
-            finish(2 * k + u, slots[u])
-
-    if count % 2 == 0:
-        multiply(count - 1, slots[1])
-        finish(count - 2, slots[0])
-    finish(count - 1, slots[(count - 1) % 2])
-
-
 def in_hbm(values):
     return pltpu.with_memory_space_constraint(values, pltpu.HBM)
 
@@ -91,7 +76,7 @@
     far_rows,
     near_cols,
     far_cols,
-    gain_ref,
+    gain_hbm,
     first_hbm,
     second_hbm,
     in_proj_hbm,
@@ -114,6 +99,7 @@
     first_ref,
     second_ref,
     in_ref,
+    gain_ref,
     sems,
 ):
     rows, cols, channels = cur_ref.shape
@@ -123,14 +109,17 @@
             ((first_hbm, first_ref), (second_hbm, second_ref), (in_proj_hbm, in_ref))
         )
     ]
+    gain_copy = pltpu.make_async_copy(gain_hbm.at[layer], gain_ref, sems.at[3])
+    gain_copy.start()
     for copy in feed:
         copy.start()
     half = channels // 2
     near_top = parity("row") == 1
     near_left = parity("col") == 1
     edge_ref = edge_factors()
-    gain_one = gain_ref[layer, 0:1, :]
-    gain_two = gain_ref[layer, 1:2, :]
+    gain_copy.wait()
+    gain_one = gain_ref[0:1, :]
+    gain_two = gain_ref[1:2, :]
     long = rows + 2 * RIM
 
     spot = lax.broadcasted_iota(jnp.int32, (long, channels), 0)
@@ -154,23 +143,18 @@
         row = rounded(normalised(values, gain_one))
         if keep is not None:
             row = row * keep
-        spread(row, sides_ref[1, pl.ds(dst, 1)], sides_ref[2, pl.ds(dst, 1)], one_ref, dst, cols)
-        left_side[pl.ds(dst, 1), 2 * channels : 3 * channels] = row[0:1]
-        right_side[pl.ds(dst, 1), 0:channels] = row[cols - 1 : cols]
-
-    for r in range(RIM):
-        norm_row(chosen(near_top, 0, near_rows[r], far_rows[r]), r, edge_ref[0])
-        norm_row(chosen(near_top, 1, near_rows[r], far_rows[r]), RIM + rows + r, edge_ref[1])
-
-    unroll = largest_divisor(rows, 4)
-
-    @pl.loop(0, rows // unroll)
-    def _(step):
-        for u in range(unroll):
-            i = step * unroll + u
-            norm_row(cur_ref[i].astype(jnp.float32), i + RIM)
-
-    feed[0].wait()
+        spread(row, sides_ref[1, dst : dst + 1], sides_ref[2, dst : dst + 1], one_ref, dst, cols)
+        left_side[dst : dst + 1, 2 * channels : 3 * channels] = row[0:1]
+        right_side[dst : dst + 1, 0:channels] = row[cols - 1 : cols]
+
+    def norm_any(dst):
+        if dst < RIM:
+            norm_row(chosen(near_top, 0, near_rows[dst], far_rows[dst]), dst, edge_ref[0])
+        elif dst < RIM + rows:
+            norm_row(cur_ref[dst - RIM].astype(jnp.float32), dst)
+        else:
+            r = dst - RIM - rows
+            norm_row(chosen(near_top, 1, near_rows[r], far_rows[r]), dst, edge_ref[1])
 
     def windows(src_ref, base, count):
         return jnp.concatenate(
@@ -182,40 +166,38 @@
         )
 
     tall = rows + 2
-    padded = left_one.shape[0]
-    place = lax.broadcasted_iota(jnp.int32, (padded, channels), 0)
-    inside = jnp.where(place == 0, edge_ref[0], 1.0)
-    inside = jnp.where(place == tall - 1, edge_ref[1], inside)
     group = slot_a.shape[0] // cols
+    first_steps = tall // group
+    ends = -(-group // 16) * 16
 
     def first_multiply(g, slot):
-        window = windows(one_ref, g * group, group)
-        if isinstance(g, int) and g == 0:
-            sides = [
-                jnp.concatenate([side[a : a + padded] for a in range(3)], axis=1)
-                for side in (left_side, right_side)
-            ]
-            window = jnp.concatenate([window] + [v.astype(jnp.bfloat16) for v in sides], axis=0)
+        base = g * group
+        sides = [
+            jnp.concatenate([side[base + a : base + a + ends] for a in range(3)], axis=1)
+            for side in (left_side, right_side)
+        ]
+        window = jnp.concatenate(
+            [windows(one_ref, base, group)] + [v.astype(jnp.bfloat16) for v in sides], axis=0
+        )
         total = jnp.dot(window, first_ref[...], preferred_element_type=jnp.float32)
         slot[...] = total[: group * cols]
-        if isinstance(g, int) and g == 0:
-            for k, one_side in enumerate((left_one, right_one)):
-                start = group * cols + k * padded
-                one_side[...] = rounded(
-                    gelu(total[start : start + padded]) * (inside * edge_ref[2 + k])
-                )
+        place = lax.broadcasted_iota(jnp.int32, (ends, channels), 0) + base
+        inside = jnp.where(place == 0, edge_ref[0], jnp.where(place == tall - 1, edge_ref[1], 1.0))
+        for k, one_side in enumerate((left_one, right_one)):
+            start = group * cols + k * ends
+            part = rounded(gelu(total[start : start + ends]) * (inside * edge_ref[2 + k]))
+            one_side[base : base + group] = part[:group]
 
     def first_finish(g, slot):
         for u in range(group):
             i = g * group + u
-            keep = jnp.where(i == 0, edge_ref[0], jnp.where(i == tall - 1, edge_ref[1], 1.0))
-            row = rounded(gelu(slot[u * cols : (u + 1) * cols])) * keep
-            spread(row, left_one[pl.ds(i, 1)], right_one[pl.ds(i, 1)], two_ref, i, cols)
-
-    pipelined(tall // group, first_multiply, first_finish, (slot_a, slot_b))
-
-    feed[1].wait()
-    feed[2].wait()
+            row = rounded(gelu(slot[u * cols : (u + 1) * cols]))
+            if i == 0:
+                row = row * edge_ref[0]
+            if i == tall - 1:
+                row = row * edge_ref[1]
+            spread(row, left_one[i : i + 1], right_one[i : i + 1], two_ref, i, cols)
+
     many = slot_c.shape[0] // cols
 
     def second_multiply(g, slot):
@@ -226,7 +208,7 @@
         )
 
     def second_finish(g, slot):
-        where = pl.ds(pl.multiple_of(g * many * cols, many * cols), many * cols)
+        where = slice(g * many * cols, (g + 1) * many * cols)
         total = slot[...] + cur_ref[pl.ds(g * many, many)].reshape(
             many * cols, channels
         ).astype(jnp.float32)
@@ -238,15 +220,39 @@
         for k, out in enumerate((lu_ref, lv_ref, gu_ref, gv_ref)):
             out[where] = expanded[:, k * half : (k + 1) * half]
 
-    pipelined(rows // many, second_multiply, second_finish, (slot_c, slot_d))
+    second_steps = rows // many
+    slots = (slot_a, slot_b)
+    others = (slot_c, slot_d)
+
+    def norm_group(g):
+        begin = 0 if g == 0 else g * group + 2
+        for dst in range(begin, (g + 1) * group + 2):
+            norm_any(dst)
+
+    norm_group(0)
+    feed[0].wait()
+    for g in range(first_steps):
+        first_multiply(g, slots[g % 2])
+        if g > 0:
+            first_finish(g - 1, slots[(g - 1) % 2])
+        if g + 1 < first_steps:
+            norm_group(g + 1)
+    feed[1].wait()
+    feed[2].wait()
+    second_multiply(0, others[0])
+    first_finish(first_steps - 1, slots[(first_steps - 1) % 2])
+    for g in range(1, second_steps):
+        second_multiply(g, others[g % 2])
+        second_finish(g - 1, others[(g - 1) % 2])
+    second_finish(second_steps - 1, others[(second_steps - 1) % 2])
+
 
 def front(layer, cur, rim_rows, rim_cols, gains, first, second, proj):
     rows, cols, channels = cur.shape
     pixels = rows * cols
     half = channels // 2
     long = rows + 2 * RIM
-    padded = -(-(rows + 2) // 16) * 16
-    tall = padded + 8
+    tall = -(-(rows + 2) // 16) * 16 + 16
     group = largest_divisor(rows + 2, GROUP_ONE)
     many = largest_divisor(rows, GROUP_TWO)
     bf = jnp.bfloat16
@@ -256,7 +262,7 @@
     return pl.pallas_call(
         functools.partial(front_kernel, layer),
         out_shape=outs,
-        in_specs=[VMEM] * 6 + [ANY] * 3,
+        in_specs=[VMEM] * 5 + [ANY] * 4,
         out_specs=[VMEM] * 5,
         scratch_shapes=[
             pltpu.VMEM((long, cols, 3 * channels), bf),
@@ -264,8 +270,8 @@
             pltpu.VMEM((2 * RIM, tall, channels), f32),
             pltpu.VMEM((tall, 3 * channels), f32),
             pltpu.VMEM((tall, 3 * channels), f32),
-            pltpu.VMEM((padded, channels), f32),
-            pltpu.VMEM((padded, channels), f32),
+            pltpu.VMEM((rows + 2, channels), f32),
+            pltpu.VMEM((rows + 2, channels), f32),
             pltpu.VMEM((group * cols, channels), f32),
             pltpu.VMEM((group * cols, channels), f32),
             pltpu.VMEM((many * cols, channels), f32),
@@ -273,7 +279,8 @@
             pltpu.VMEM(first.shape[1:], bf),
             pltpu.VMEM(second.shape[1:], bf),
             pltpu.VMEM(proj.shape[1:], bf),
-            pltpu.SemaphoreType.DMA((3,)),
+            pltpu.VMEM(gains.shape[1:], f32),
+            pltpu.SemaphoreType.DMA((4,)),
         ],
         compiler_params=pltpu.CompilerParams(vmem_limit_bytes=34 * MIB),
         cost_estimate=pl.CostEstimate(
@@ -282,7 +289,7 @@
             transcendentals=3 * pixels * channels,
         ),
         name="front",
-    )(cur, *rim_rows, *rim_cols, gains, *(in_hbm(w) for w in (first, second, proj)))
+    )(cur, *rim_rows, *rim_cols, *(in_hbm(w) for w in (gains, first, second, proj)))
 
 
 def local_kernel(
@@ -369,8 +376,8 @@
             else:
                 out_ref[:, part] = blend.reshape(cells, tile, half).astype(jnp.bfloat16)
 
+
 def grid_mixing(got, mix, bias):
-    cells, share, half = got.shape
     return pl.pallas_call(
         grid_kernel,
         out_shape=jax.ShapeDtypeStruct(got.shape, jnp.bfloat16),
@@ -458,7 +465,7 @@
 
 def strips_kernel(image_hbm, cur_ref, *refs):
     *strip_refs, strip_ref, sem = refs
-    rows, cols, channels = image_hbm.shape
+    rows, cols, _ = image_hbm.shape
     copy = pltpu.make_async_copy(image_hbm, cur_ref, sem.at[0])
     copy.start()
     copy.wait()
@@ -473,7 +480,7 @@
 
 
 def strips(image):
-    rows, cols, channels = image.shape
+    rows, _, channels = image.shape
     return pl.pallas_call(
         strips_kernel,
         out_shape=[jax.ShapeDtypeStruct(image.shape, jnp.bfloat16)] + strip_shapes(image.shape),
@@ -488,10 +495,10 @@
     )(in_hbm(image))
 
 
-def traded(axis, near, far):
+def traded(axis, near, far, around):
     count = lax.axis_size(axis)
     inner = [(i, i ^ 1) for i in range(count)]
-    outer = [(i, (i + 1) % count) for i in range(1, count, 2)]
+    outer = [(i, (i + 1) % count) for i in range(1, count if around else count - 1, 2)]
     outer += [(target, source) for source, target in outer]
     far = lax.ppermute(far, axis, outer)
     near = lax.ppermute(near, axis, inner)
@@ -500,7 +507,7 @@
 
 def columns_kernel(near_rows, far_rows, left_ref, right_ref, near_ref, far_ref):
     odd_row, odd_col = parity("row"), parity("col")
-    rim, rows, _ = left_ref.shape
+    rim, _, _ = left_ref.shape
     cols = near_rows.shape[1]
     near_top = odd_row == 1
     for side, own_ref in ((0, left_ref), (1, right_ref)):
@@ -545,8 +552,8 @@
 
 
 def rims(near_rows, far_rows, left, right):
-    rim_rows = traded("row", near_rows, far_rows)
-    return rim_rows, traded("col", *columns(*rim_rows, left, right))
+    rim_rows = traded("row", near_rows, far_rows, True)
+    return rim_rows, traded("col", *columns(*rim_rows, left, right), False)
 
 
 def on_device(
@@ -589,13 +596,9 @@
             tile,
         )
         gv, gl = lax.optimization_barrier((gv, gl))
-        got = lax.all_to_all(
-            gv.reshape(1, cells, share, half), ("row", "col"), 1, 0, tiled=True
-        )
+        got = lax.all_to_all(gv.reshape(1, cells, share, half), ("row", "col"), 1, 0, tiled=True)
         blend = grid_mixing(got.reshape(cells, share, half), mix_tiles, bias_tiles)
-        gm = lax.all_to_all(
-            blend.reshape(cells, 1, share, half), ("row", "col"), 0, 1, tiled=True
-        )
+        gm = lax.all_to_all(blend.reshape(cells, 1, share, half), ("row", "col"), 0, 1, tiled=True)
         current, *own = back(
             layer,
             last,

time: 163 us -> 157 us (0.963)
  blocking collectives: 98.5 us -> 106 us
  waiting for transfers between devices: 12 us -> 6.39 us
  Pallas kernels: 40 us -> 34.9 us
    all_to_all x2, blocking collectives: 51 us -> 58.3 us  [on_device(): lax.all_to_all(gv.reshape(1, cells, share, half), ('row', 'col'), 1, 0, t...]
    ppermute x4, waiting for transfers between devices: 11.2 us -> 4.74 us  [traded(): far = lax.ppermute(far, axis, outer)]
    pallas_call x2, Pallas kernels: 31.7 us -> 26.8 us  [front(): pl.pallas_call(functools.partial(front_kernel, layer), out_shape=outs, in...]
  transfers between devices with their start and end apart: 8 -> 8, of which waited for: 5 -> 4; matrix products, arithmetic and copies ran while one was open for 0% -> 0% of each run, Pallas kernels for 0% -> 0%
where the time goes in v1:
time: 157 us
  blocking collectives  106 us (68%)
  Pallas kernels  34.9 us (22%)
  starting transfers between devices  9.71 us (6%)
  waiting for transfers between devices  6.39 us (4%)
    all_to_all x2, blocking collectives, on_device(): lax.all_to_all(gv.reshape(1, cells, share, half), ('row', 'col'), 1, 0, t...  58.3 us
    all_to_all x2, blocking collectives, on_device(): lax.all_to_all(blend.reshape(cells, 1, share, half), ('row', 'col'), 0, 1...  47.5 us
    pallas_call x2, Pallas kernels, front(): pl.pallas_call(functools.partial(front_kernel, layer), out_shape=outs, in...  26.8 us
    ppermute x4, starting transfers between devices, traded(): far = lax.ppermute(far, axis, outer)  5.7 us
    ppermute x4, waiting for transfers between devices, traded(): far = lax.ppermute(far, axis, outer)  4.74 us
    ppermute x4, starting transfers between devices, traded(): near = lax.ppermute(near, axis, inner)  4.01 us
    pallas_call x2, Pallas kernels, back(): pl.pallas_call(functools.partial(back_kernel, layer, last), out_shape=out...  4 us
  transfers between devices with their start and end apart: 8, of which 4 were waited for; matrix products, arithmetic and copies ran while one was open for 0% of the time, Pallas kernels for 0%

profile of v1, /device:TPU:1, one launch (start us, length us, event | category | flops | bytes accessed | tf_op | source)
XLA Modules:
  0.0 157.0 jit_solution(13229888668651318773)
XLA Ops:
  0.0 1.5 strips.1
  1.6 0.1 collective-permute-start
  1.6 2.6 %collective-permute-start.1 = (bf16[2,64,256]{2,1,0:T(8,128)(2,1)S(1)}, bf16[2,64,256]{2,1,0:T(8,128)(2,1)S(1)}, u32[]{:S(2)}, u32[]{:S(2)}) collective-permute-start(bf16[2,64,256]{2,1,0:T(8,128)(2,1)S(1)} %get-tuple-element.41), channel_id=1, source_target_pairs={{4,8},{12,16},{20,24},{28,0},{8,4},{16,12},{24,20},{0,28},{5,9},{1... | collective-permute-start | bytes 196616 | tf_op jit(solution)/shard_map/ppermute | solution.py:503
  4.3 0.0 collective-permute-done.near_rows
  4.3 2.2 %collective-permute-done.1.far_rows = bf16[2,64,256]{2,1,0:T(8,128)(2,1)S(1)} collective-permute-done((bf16[2,64,256]{2,1,0:T(8,128)(2,1)S(1)}, bf16[2,64,256]{2,1,0:T(8,128)(2,1)S(1)}, u32[]{:S(2)}, u32[]{:S(2)}) %collective-permute-start.1) | collective-permute-done | bytes 65568 | tf_op jit(solution)/shard_map/ppermute | solution.py:503
  6.6 2.2 %collective-permute-start.2 = (bf16[2,52,256]{2,1,0:T(8,128)(2,1)S(1)}, bf16[2,52,256]{2,1,0:T(8,128)(2,1)S(1)}, u32[]{:S(2)}, u32[]{:S(2)}) collective-permute-start(bf16[2,52,256]{2,1,0:T(8,128)(2,1)S(1)} %get-tuple-element.44), channel_id=1, source_target_pairs={{0,1},{1,0},{2,3},{3,2},{4,5},{5,4},{6,7},{7,6},{8,9},{9,8},{10,11... | collective-permute-start | bytes 159752 | tf_op jit(solution)/shard_map/ppermute | solution.py:504
  8.8 0.7 collective-permute-start.3
  9.5 0.9 collective-permute-done.2.near_cols
  10.4 0.0 collective-permute-done.3.far_cols
  10.4 0.0 copy-start.1
  10.4 0.0 copy-start.2
  10.4 0.0 copy-start.3
  10.4 0.0 copy-start.4
  10.4 13.4 %front.2 = (f32[3072,256]{1,0:T(8,128)S(1)}, bf16[3072,128]{1,0:T(8,128)(2,1)S(1)}, bf16[3072,128]{1,0:T(8,128)(2,1)S(1)}, bf16[3072,128]{1,0:T(8,128)(2,1)S(1)}, bf16[3072,128]{1,0:T(8,128)(2,1)S(1)}) custom-call(bf16[48,64,256]{2,1,0:T(8,128)(2,1)S(1)} %get-tuple-element.39.cur_ref, bf16[2,64,256]{2,1,0:T(8,128)(2,1)S(1)} %collective-permute-done.near_rows, ...), custom_call_target="tpu_custom_call" | custom-call | flops 8053063680 | bytes 12582912 | tf_op jit(solution)/shard_map/front/pallas_call | solution.py:262
  23.8 0.0 copy-done.1
  23.9 0.0 copy-done.2
  23.9 0.0 copy-done.3
  23.9 0.0 copy-done.4
  23.9 0.7 local.2
  24.5 30.1 %all_to_all.16 = bf16[1,32,96,128]{3,2,0,1:T(8,128)(2,1)S(1)} all-to-all(bf16[1,32,96,128]{3,2,0,1:T(8,128)(2,1)S(1)} %bitcast.31), channel_id=1, replica_groups=mesh['row'=8,'col'=4] {'row','col'}, dimensions={1} | all-to-all | bytes 1572864 | tf_op jit(solution)/shard_map/all_to_all | solution.py:599
  54.6 0.0 copy-start
  54.6 0.6 grid_mixing.2
  55.2 23.8 %all_to_all.17 = bf16[32,1,96,128]{3,2,1,0:T(8,128)(2,1)S(1)} all-to-all(bf16[32,1,96,128]{3,2,1,0:T(8,128)(2,1)S(1)} %bitcast.27), channel_id=1, replica_groups=mesh['row'=8,'col'=4] {'row','col'}, dimensions={0} | all-to-all | bytes 1572864 | tf_op jit(solution)/shard_map/all_to_all | solution.py:601
  79.0 0.0 copy-done
  79.0 1.5 back.2
  80.5 0.1 collective-permute-start.4
  80.6 1.6 collective-permute-start.5
  82.1 0.0 collective-permute-done.4.near_rows
  82.1 2.5 %collective-permute-done.5.far_rows = bf16[2,64,256]{2,1,0:T(8,128)(2,1)S(1)} collective-permute-done((bf16[2,64,256]{2,1,0:T(8,128)(2,1)S(1)}, bf16[2,64,256]{2,1,0:T(8,128)(2,1)S(1)}, u32[]{:S(2)}, u32[]{:S(2)}) %collective-permute-start.5) | collective-permute-done | bytes 65568 | tf_op jit(solution)/shard_map/ppermute | solution.py:503
  84.7 1.6 %collective-permute-start.6 = (bf16[2,52,256]{2,1,0:T(8,128)(2,1)S(1)}, bf16[2,52,256]{2,1,0:T(8,128)(2,1)S(1)}, u32[]{:S(2)}, u32[]{:S(2)}) collective-permute-start(bf16[2,52,256]{2,1,0:T(8,128)(2,1)S(1)} %get-tuple-element.61), channel_id=1, source_target_pairs={{0,1},{1,0},{2,3},{3,2},{4,5},{5,4},{6,7},{7,6},{8,9},{9,8},{10,11... | collective-permute-start | bytes 159752 | tf_op jit(solution)/shard_map/ppermute | solution.py:504
  86.3 0.8 collective-permute-start.7
  87.1 0.7 collective-permute-done.6.near_cols
  87.9 0.0 collective-permute-done.7.far_cols
  87.9 13.4 %front.3 = (f32[3072,256]{1,0:T(8,128)S(1)}, bf16[3072,128]{1,0:T(8,128)(2,1)S(1)}, bf16[3072,128]{1,0:T(8,128)(2,1)S(1)}, bf16[3072,128]{1,0:T(8,128)(2,1)S(1)}, bf16[3072,128]{1,0:T(8,128)(2,1)S(1)}) custom-call(bf16[48,64,256]{2,1,0:T(8,128)(2,1)S(1)} %get-tuple-element.56.cur_ref, bf16[2,64,256]{2,1,0:T(8,128)(2,1)S(1)} %collective-permute-done.4.near_rows, ...), custom_call_target="tpu_custom_call" | custom-call | flops 8053063680 | bytes 12582912 | tf_op jit(solution)/shard_map/front/pallas_call | solution.py:262
  101.2 0.7 local.3
  101.9 28.2 %all_to_all.18 = bf16[1,32,96,128]{3,2,0,1:T(8,128)(2,1)S(1)} all-to-all(bf16[1,32,96,128]{3,2,0,1:T(8,128)(2,1)S(1)} %bitcast.32), channel_id=1, replica_groups=mesh['row'=8,'col'=4] {'row','col'}, dimensions={1} | all-to-all | bytes 1572864 | tf_op jit(solution)/shard_map/all_to_all | solution.py:599
  130.2 0.6 grid_mixing.3
  130.7 23.8 %all_to_all.19 = bf16[32,1,96,128]{3,2,1,0:T(8,128)(2,1)S(1)} all-to-all(bf16[32,1,96,128]{3,2,1,0:T(8,128)(2,1)S(1)} %bitcast.28), channel_id=1, replica_groups=mesh['row'=8,'col'=4] {'row','col'}, dimensions={0} | all-to-all | bytes 1572864 | tf_op jit(solution)/shard_map/all_to_all | solution.py:601
  154.5 2.5 %back.3 = bf16[48,64,256]{2,1,0:T(8,128)(2,1)} custom-call(f32[3072,256]{1,0:T(8,128)S(1)} %get-tuple-element.63.mixed_ref, bf16[3072,128]{1,0:T(8,128)(2,1)S(1)} %bitcast.30, bf16[3072,128]{1,0:T(8,128)(2,1)S(1)} %get-tuple-element.69.gu_ref, bf16[3072,128]{1,0:T(8,128)(2,1)S(1)} %bitcast.24, bf16[2,256,256]{2,1,0:T(8,128)(2,1)S(1)} %copy-done), custom_call_target="tpu_custom_call" | custom-call | flops 402653184 | bytes 7077888 | tf_op jit(solution)/shard_map/back/pallas_call | solution.py:450
  (2 shorter events, 0.1 us)
Async XLA Ops:
  1.6 2.7 %collective-permute-start = (bf16[2,64,256]{2,1,0:T(8,128)(2,1)S(1)}, bf16[2,64,256]{2,1,0:T(8,128)(2,1)S(1)}, u32[]{:S(2)}, u32[]{:S(2)}) collective-permute-start(bf16[2,64,256]{2,1,0:T(8,128)(2,1)S(1)} %get-tuple-element.40), channel_id=1, source_target_pairs={{0,4},{4,0},{8,12},{12,8},{16,20},{20,16},{24,28},{28,24},{1,5},{5... | collective-permute-start | bytes 196616 | tf_op jit(solution)/shard_map/ppermute | solution.py:504
  1.6 4.9 %collective-permute-start.1 = (bf16[2,64,256]{2,1,0:T(8,128)(2,1)S(1)}, bf16[2,64,256]{2,1,0:T(8,128)(2,1)S(1)}, u32[]{:S(2)}, u32[]{:S(2)}) collective-permute-start(bf16[2,64,256]{2,1,0:T(8,128)(2,1)S(1)} %get-tuple-element.41), channel_id=1, source_target_pairs={{4,8},{12,16},{20,24},{28,0},{8,4},{16,12},{24,20},{0,28},{5,9},{1... | collective-permute-start | bytes 196616 | tf_op jit(solution)/shard_map/ppermute | solution.py:503
  6.6 3.8 %collective-permute-start.2 = (bf16[2,52,256]{2,1,0:T(8,128)(2,1)S(1)}, bf16[2,52,256]{2,1,0:T(8,128)(2,1)S(1)}, u32[]{:S(2)}, u32[]{:S(2)}) collective-permute-start(bf16[2,52,256]{2,1,0:T(8,128)(2,1)S(1)} %get-tuple-element.44), channel_id=1, source_target_pairs={{0,1},{1,0},{2,3},{3,2},{4,5},{5,4},{6,7},{7,6},{8,9},{9,8},{10,11... | collective-permute-start | bytes 159752 | tf_op jit(solution)/shard_map/ppermute | solution.py:504
  8.8 1.6 %collective-permute-start.3 = (bf16[2,52,256]{2,1,0:T(8,128)(2,1)S(1)}, bf16[2,52,256]{2,1,0:T(8,128)(2,1)S(1)}, u32[]{:S(2)}, u32[]{:S(2)}) collective-permute-start(bf16[2,52,256]{2,1,0:T(8,128)(2,1)S(1)} %get-tuple-element.45), channel_id=1, source_target_pairs={{1,2},{2,1},{5,6},{6,5},{9,10},{10,9},{13,14},{14,13},{17,18},{18,... | collective-permute-start | bytes 159752 | tf_op jit(solution)/shard_map/ppermute | solution.py:503
  10.4 13.4 %copy-start.1 = (bf16[2,256,256]{2,1,0:T(8,128)(2,1)S(1)}, bf16[2,256,256]{2,1,0:T(8,128)(2,1)}, u32[]{:S(2)}) copy-start(bf16[2,256,256]{2,1,0:T(8,128)(2,1)} %mix_ref.3) | copy-start | bytes 786436
  10.4 13.5 %copy-start.2 = (bf16[2,32,32]{2,1,0:T(8,128)(2,1)S(1)}, bf16[2,32,32]{2,1,0:T(8,128)(2,1)}, u32[]{:S(2)}) copy-start(bf16[2,32,32]{2,1,0:T(8,128)(2,1)} %grid_ref.3) | copy-start | bytes 12292
  10.4 13.5 %copy-start.3 = (f32[2,256]{1,0:T(2,128)S(1)}, f32[2,256]{1,0:T(2,128)}, u32[]{:S(2)}) copy-start(f32[2,256]{1,0:T(2,128)} %bias_ref.3) | copy-start | bytes 6148
  10.4 13.5 %copy-start.4 = (f32[2,32]{1,0:T(2,128)S(1)}, f32[2,32]{1,0:T(2,128)}, u32[]{:S(2)}) copy-start(f32[2,32]{1,0:T(2,128)} %grid_bias_ref.3) | copy-start | bytes 772
  54.6 24.3 %copy-start = (bf16[2,256,256]{2,1,0:T(8,128)(2,1)S(1)}, bf16[2,256,256]{2,1,0:T(8,128)(2,1)}, u32[]{:S(2)}) copy-start(bf16[2,256,256]{2,1,0:T(8,128)(2,1)} %proj_ref.3) | copy-start | bytes 786436
  80.5 1.6 %collective-permute-start.4 = (bf16[2,64,256]{2,1,0:T(8,128)(2,1)S(1)}, bf16[2,64,256]{2,1,0:T(8,128)(2,1)S(1)}, u32[]{:S(2)}, u32[]{:S(2)}) collective-permute-start(bf16[2,64,256]{2,1,0:T(8,128)(2,1)S(1)} %get-tuple-element.57), channel_id=1, source_target_pairs={{0,4},{4,0},{8,12},{12,8},{16,20},{20,16},{24,28},{28,24},{1,5},{5... | collective-permute-start | bytes 196616 | tf_op jit(solution)/shard_map/ppermute | solution.py:504
  80.6 4.1 %collective-permute-start.5 = (bf16[2,64,256]{2,1,0:T(8,128)(2,1)S(1)}, bf16[2,64,256]{2,1,0:T(8,128)(2,1)S(1)}, u32[]{:S(2)}, u32[]{:S(2)}) collective-permute-start(bf16[2,64,256]{2,1,0:T(8,128)(2,1)S(1)} %get-tuple-element.58), channel_id=1, source_target_pairs={{4,8},{12,16},{20,24},{28,0},{8,4},{16,12},{24,20},{0,28},{5,9},{1... | collective-permute-start | bytes 196616 | tf_op jit(solution)/shard_map/ppermute | solution.py:503
  84.7 3.2 %collective-permute-start.6 = (bf16[2,52,256]{2,1,0:T(8,128)(2,1)S(1)}, bf16[2,52,256]{2,1,0:T(8,128)(2,1)S(1)}, u32[]{:S(2)}, u32[]{:S(2)}) collective-permute-start(bf16[2,52,256]{2,1,0:T(8,128)(2,1)S(1)} %get-tuple-element.61), channel_id=1, source_target_pairs={{0,1},{1,0},{2,3},{3,2},{4,5},{5,4},{6,7},{7,6},{8,9},{9,8},{10,11... | collective-permute-start | bytes 159752 | tf_op jit(solution)/shard_map/ppermute | solution.py:504
  86.3 1.6 %collective-permute-start.7 = (bf16[2,52,256]{2,1,0:T(8,128)(2,1)S(1)}, bf16[2,52,256]{2,1,0:T(8,128)(2,1)S(1)}, u32[]{:S(2)}, u32[]{:S(2)}) collective-permute-start(bf16[2,52,256]{2,1,0:T(8,128)(2,1)S(1)} %get-tuple-element.62), channel_id=1, source_target_pairs={{1,2},{2,1},{5,6},{6,5},{9,10},{10,9},{13,14},{14,13},{17,18},{18,... | collective-permute-start | bytes 159752 | tf_op jit(solution)/shard_map/ppermute | solution.py:503

commit v2 on v1

--- a/solution.py
+++ b/solution.py
@@ -292,9 +292,7 @@
     )(cur, *rim_rows, *rim_cols, *(in_hbm(w) for w in (gains, first, second, proj)))
 
 
-def local_kernel(
-    layer, lu_ref, lv_ref, mix_ref, bias_ref, grid_ref, grid_bias_ref, out_ref, tiles_ref, shift_ref
-):
+def local_kernel(layer, lu_ref, lv_ref, mix_ref, bias_ref, out_ref):
     rows, cols, half = lu_ref.shape
     down, across = rows // BLOCK, cols // BLOCK
     pair = 2 if across % 2 == 0 else 1
@@ -314,35 +312,51 @@
                 u = lu_ref[r, c].reshape(BLOCK * BLOCK, half).astype(jnp.float32)
                 gated = (u * m[:, k * half : (k + 1) * half]).astype(jnp.bfloat16)
                 out_ref[r, c] = gated.reshape(BLOCK, BLOCK, half)
+
+
+def tiles_kernel(grid_ref, grid_bias_ref, tiles_ref, shift_ref):
     cells = grid_ref.shape[-1]
-    wide = tiles_ref.shape[0]
+    wide = tiles_ref.shape[1]
     tile = wide // cells
     down_of = lax.broadcasted_iota(jnp.int32, (wide, cells), 0) // tile
     chosen = down_of == lax.broadcasted_iota(jnp.int32, (wide, cells), 1)
-    shift = jnp.sum(jnp.where(chosen, grid_bias_ref[layer : layer + 1], 0.0), axis=1, keepdims=True)
-    shift_ref[...] = jnp.broadcast_to(shift, shift_ref.shape)
-    pick = chosen.astype(jnp.bfloat16)
-    across_of = lax.broadcasted_iota(jnp.int32, (cells, wide), 1) // tile
-    lay = (across_of == lax.broadcasted_iota(jnp.int32, (cells, wide), 0)).astype(jnp.bfloat16)
-    tall = jnp.dot(pick, grid_ref[layer], preferred_element_type=jnp.float32)
-    full = jnp.dot(tall.astype(jnp.bfloat16), lay, preferred_element_type=jnp.float32)
-    p = lax.broadcasted_iota(jnp.int32, (wide, wide), 0) % tile
-    q = lax.broadcasted_iota(jnp.int32, (wide, wide), 1) % tile
-    tiles_ref[...] = jnp.where(p == q, full, 0.0).astype(jnp.bfloat16)
-
-
-def local(layer, lu, lv, mix, bias, grid, grid_bias, tile):
+    for layer in range(grid_ref.shape[0]):
+        shift = jnp.sum(jnp.where(chosen, grid_bias_ref[layer : layer + 1], 0.0), axis=1, keepdims=True)
+        shift_ref[layer] = jnp.broadcast_to(shift, shift_ref.shape[1:])
+        pick = chosen.astype(jnp.bfloat16)
+        across_of = lax.broadcasted_iota(jnp.int32, (cells, wide), 1) // tile
+        lay = (across_of == lax.broadcasted_iota(jnp.int32, (cells, wide), 0)).astype(jnp.bfloat16)
+        tall = jnp.dot(pick, grid_ref[layer], preferred_element_type=jnp.float32)
+        full = jnp.dot(tall.astype(jnp.bfloat16), lay, preferred_element_type=jnp.float32)
+        p = lax.broadcasted_iota(jnp.int32, (wide, wide), 0) % tile
+        q = lax.broadcasted_iota(jnp.int32, (wide, wide), 1) % tile
+        tiles_ref[layer] = jnp.where(p == q, full, 0.0).astype(jnp.bfloat16)
+
+
+def mixing_tiles(grid, grid_bias, tile, half):
+    layers, cells, _ = grid.shape
+    wide = cells * tile
+    return pl.pallas_call(
+        tiles_kernel,
+        out_shape=[
+            jax.ShapeDtypeStruct((layers, wide, wide), jnp.bfloat16),
+            jax.ShapeDtypeStruct((layers, wide, half), jnp.float32),
+        ],
+        in_specs=[VMEM] * 2,
+        out_specs=[VMEM] * 2,
+        compiler_params=pltpu.CompilerParams(vmem_limit_bytes=24 * MIB),
+        cost_estimate=pl.CostEstimate(flops=0, bytes_accessed=4 * MIB, transcendentals=0),
+        name="mixing_tiles",
+    )(grid, grid_bias)
+
+
+def local(layer, lu, lv, mix, bias):
     rows, cols, half = lu.shape
-    wide = grid.shape[-1] * tile
     return pl.pallas_call(
         functools.partial(local_kernel, layer),
-        out_shape=[
-            jax.ShapeDtypeStruct(lu.shape, jnp.bfloat16),
-            jax.ShapeDtypeStruct((wide, wide), jnp.bfloat16),
-            jax.ShapeDtypeStruct((wide, half), jnp.float32),
-        ],
-        in_specs=[VMEM] * 6,
-        out_specs=[VMEM] * 3,
+        out_shape=jax.ShapeDtypeStruct(lu.shape, jnp.bfloat16),
+        in_specs=[VMEM] * 4,
+        out_specs=VMEM,
         compiler_params=pltpu.CompilerParams(vmem_limit_bytes=12 * MIB),
         cost_estimate=pl.CostEstimate(
             flops=2 * rows * cols * half * BLOCK * BLOCK,
@@ -350,12 +364,12 @@
             transcendentals=0,
         ),
         name="local",
-    )(lu, lv, mix, bias, grid, grid_bias)
-
-
-def grid_kernel(got_ref, mix_ref, bias_ref, out_ref):
+    )(lu, lv, mix, bias)
+
+
+def grid_kernel(layer, got_ref, mix_ref, bias_ref, out_ref):
     cells, share, half = got_ref.shape
-    tile = mix_ref.shape[0] // cells
+    tile = mix_ref.shape[1] // cells
     step = 2 * tile if share % (2 * tile) == 0 else tile
     for k in range(share // step):
         parts = [slice(t, t + tile) for t in range(k * step, (k + 1) * step, tile)]
@@ -367,19 +381,19 @@
                 for part in parts
             ]
         m = jnp.dot(
-            mix_ref[...], jnp.concatenate(v, axis=1), preferred_element_type=jnp.float32
+            mix_ref[layer], jnp.concatenate(v, axis=1), preferred_element_type=jnp.float32
         )
         for n, part in enumerate(parts):
-            blend = m[:, n * half : (n + 1) * half] + bias_ref[...]
+            blend = m[:, n * half : (n + 1) * half] + bias_ref[layer]
             if tile == 16:
                 out_ref[:, part] = blend.astype(jnp.bfloat16).reshape(cells, tile, half)
             else:
                 out_ref[:, part] = blend.reshape(cells, tile, half).astype(jnp.bfloat16)
 
 
-def grid_mixing(got, mix, bias):
-    return pl.pallas_call(
-        grid_kernel,
+def grid_mixing(layer, got, mix, bias):
+    return pl.pallas_call(
+        functools.partial(grid_kernel, layer),
         out_shape=jax.ShapeDtypeStruct(got.shape, jnp.bfloat16),
         in_specs=[VMEM] * 3,
         out_specs=VMEM,
@@ -388,7 +402,7 @@
     )(got, mix, bias)
 
 
-def keep_strips(top, bottom, strip_ref, near_ref, far_ref, left_ref, right_ref):
+def keep_rows(top, bottom, near_ref, far_ref):
     odd_row = parity("row")
 
     @pl.when(odd_row == 0)
@@ -401,11 +415,18 @@
         near_ref[...] = top
         far_ref[...] = bottom
 
+
+def keep_columns(strip_ref, left_ref, right_ref):
     left_ref[...] = strip_ref[0].astype(jnp.bfloat16)
     right_ref[...] = strip_ref[1].astype(jnp.bfloat16)
 
 
-def back_kernel(layer, last, mixed_ref, gl_ref, gu_ref, gm_ref, proj_ref, cur_ref, *refs):
+def back_kernel(layer, last, mixed_ref, gl_ref, gu_ref, gm_ref, proj_ref, *refs):
+    if last:
+        out_hbm, *refs = refs
+        cur_ref = refs[0]
+    else:
+        cur_ref, *refs = refs
     rows, cols, channels = cur_ref.shape
     many = largest_divisor(rows, 8)
 
@@ -418,7 +439,10 @@
             joined, proj_ref[layer], preferred_element_type=jnp.float32
         )
         cur_ref[pl.ds(g * many, many)] = total.reshape(many, cols, channels).astype(jnp.bfloat16)
-        if not last:
+        if last:
+            part = pl.ds(g * many, many)
+            pltpu.make_async_copy(cur_ref.at[part], out_hbm.at[part], refs[1].at[0]).start()
+        else:
             strip_ref = refs[-1]
             for u in range(many):
                 for c in range(RIM):
@@ -427,9 +451,12 @@
                     strip_ref[0, c, pl.ds(g * many + u, 1)] = total[low : low + 1]
                     strip_ref[1, c, pl.ds(g * many + u, 1)] = total[high : high + 1]
 
-    if not last:
+    if last:
+        pltpu.make_async_copy(cur_ref, out_hbm, refs[1].at[0]).wait()
+    else:
         *strip_refs, strip_ref = refs
-        keep_strips(cur_ref[0:RIM], cur_ref[rows - RIM : rows], strip_ref, *strip_refs)
+        keep_rows(cur_ref[0:RIM], cur_ref[rows - RIM : rows], *strip_refs[:2])
+        keep_columns(strip_ref, *strip_refs[2:])
 
 
 def strip_shapes(shape):
@@ -443,15 +470,16 @@
     rows, cols, channels = shape
     f32 = jnp.float32
     outs = [jax.ShapeDtypeStruct(shape, jnp.bfloat16)]
-    scratch = []
-    if not last:
+    if last:
+        scratch = [pltpu.VMEM(shape, jnp.bfloat16), pltpu.SemaphoreType.DMA((1,))]
+    else:
         outs += strip_shapes(shape)
-        scratch.append(pltpu.VMEM((2, RIM, rows, channels), f32))
+        scratch = [pltpu.VMEM((2, RIM, rows, channels), f32)]
     return pl.pallas_call(
         functools.partial(back_kernel, layer, last),
         out_shape=outs,
         in_specs=[VMEM] * 5,
-        out_specs=[VMEM] * len(outs),
+        out_specs=[ANY] if last else [VMEM] * len(outs),
         scratch_shapes=scratch,
         compiler_params=pltpu.CompilerParams(vmem_limit_bytes=16 * MIB),
         cost_estimate=pl.CostEstimate(
@@ -463,8 +491,36 @@
     )(mixed, gl, gu, gm, proj)
 
 
-def strips_kernel(image_hbm, cur_ref, *refs):
-    *strip_refs, strip_ref, sem = refs
+def row_strips_kernel(image_hbm, near_ref, far_ref, edge_ref, sems):
+    rows = image_hbm.shape[0]
+    copies = [
+        pltpu.make_async_copy(image_hbm.at[0:RIM], edge_ref.at[0], sems.at[0]),
+        pltpu.make_async_copy(image_hbm.at[rows - RIM : rows], edge_ref.at[1], sems.at[1]),
+    ]
+    for copy in copies:
+        copy.start()
+    for copy in copies:
+        copy.wait()
+    keep_rows(edge_ref[0], edge_ref[1], near_ref, far_ref)
+
+
+def row_strips(image):
+    _, cols, channels = image.shape
+    return pl.pallas_call(
+        row_strips_kernel,
+        out_shape=strip_shapes(image.shape)[:2],
+        in_specs=[ANY],
+        out_specs=[VMEM] * 2,
+        scratch_shapes=[
+            pltpu.VMEM((2, RIM, cols, channels), jnp.bfloat16),
+            pltpu.SemaphoreType.DMA((2,)),
+        ],
+        compiler_params=pltpu.CompilerParams(vmem_limit_bytes=8 * MIB),
+        name="row_strips",
+    )(in_hbm(image))
+
+
+def column_strips_kernel(image_hbm, cur_ref, left_ref, right_ref, strip_ref, sem):
     rows, cols, _ = image_hbm.shape
     copy = pltpu.make_async_copy(image_hbm, cur_ref, sem.at[0])
     copy.start()
@@ -476,22 +532,24 @@
         for c in range(RIM):
             strip_ref[0, c, i : i + 1] = low[c : c + 1]
             strip_ref[1, c, i : i + 1] = high[side - RIM + c : side - RIM + c + 1]
-    keep_strips(cur_ref[0:RIM], cur_ref[rows - RIM : rows], strip_ref, *strip_refs)
-
-
-def strips(image):
+    keep_columns(strip_ref, left_ref, right_ref)
+
+
+def column_strips(image):
     rows, _, channels = image.shape
     return pl.pallas_call(
-        strips_kernel,
-        out_shape=[jax.ShapeDtypeStruct(image.shape, jnp.bfloat16)] + strip_shapes(image.shape),
+        column_strips_kernel,
+        out_shape=[jax.ShapeDtypeStruct(image.shape, jnp.bfloat16)]
+        + strip_shapes(image.shape)[2:],
         in_specs=[ANY],
-        out_specs=[VMEM] * 5,
+        out_specs=[VMEM] * 3,
         scratch_shapes=[
             pltpu.VMEM((2, RIM, rows, channels), jnp.float32),
             pltpu.SemaphoreType.DMA((1,)),
         ],
         compiler_params=pltpu.CompilerParams(vmem_limit_bytes=8 * MIB),
-        name="strips",
+        cost_estimate=pl.CostEstimate(flops=0, bytes_accessed=8 * MIB, transcendentals=0),
+        name="column_strips",
     )(in_hbm(image))
 
 
@@ -578,26 +636,26 @@
     tile = math.gcd(share, 16)
     first = conv_first.reshape(LAYERS, 9 * channels, channels)
     second = conv_second.reshape(LAYERS, 9 * channels, channels)
-    current, *own = strips(image)
+    near_rows, far_rows = row_strips(image)
+    current, left, right = column_strips(image)
+    mix_tiles, bias_tiles = mixing_tiles(grid_mix, grid_bias, tile, half)
+    own = (near_rows, far_rows, left, right)
     for layer in range(LAYERS):
         last = layer == LAYERS - 1
         rim_rows, rim_cols = rims(*own)
         mixed, lu, lv, gu, gv = front(
             layer, current, rim_rows, rim_cols, norm_gain, first, second, proj_in
         )
-        gl, mix_tiles, bias_tiles = local(
+        gl = local(
             layer,
             lu.reshape(rows, cols, half),
             lv.reshape(rows, cols, half),
             block_mix,
             block_bias,
-            grid_mix,
-            grid_bias,
-            tile,
         )
         gv, gl = lax.optimization_barrier((gv, gl))
         got = lax.all_to_all(gv.reshape(1, cells, share, half), ("row", "col"), 1, 0, tiled=True)
-        blend = grid_mixing(got.reshape(cells, share, half), mix_tiles, bias_tiles)
+        blend = grid_mixing(layer, got.reshape(cells, share, half), mix_tiles, bias_tiles)
         gm = lax.all_to_all(blend.reshape(cells, 1, share, half), ("row", "col"), 0, 1, tiled=True)
         current, *own = back(
             layer,

time: 157 us -> 159 us (1.013)
  blocking collectives: 106 us -> 75.8 us
  waiting for transfers between devices: 6.39 us -> 24.9 us
  starting transfers between devices: 9.71 us -> 19.2 us
  local copies, waits for them, and re-layouts: 0.02 us -> 2.13 us
    all_to_all x2 -> x1, blocking collectives: 58.3 us -> 28.3 us  [on_device(): lax.all_to_all(gv.reshape(1, cells, share, half), ('row', 'col'), 1, 0, t...]
    all_to_all x0 -> x1, waiting for transfers between devices: none -> 20.1 us  [on_device(): lax.all_to_all(gv.reshape(1, cells, share, half), ('row', 'col'), 1, 0, t...]
    all_to_all x0 -> x1, starting transfers between devices: none -> 9.49 us  [on_device(): lax.all_to_all(gv.reshape(1, cells, share, half), ('row', 'col'), 1, 0, t...]
    unnamed x10 -> x18, local copies, waits for them, and re-layouts: 0.02 us -> 2.13 us
    pallas_call x5 -> x7, Pallas kernels: 3.99 us -> 5 us  [the longest x1 1.53 us: column_strips(): pl.pallas_call(column_strips_kernel, out_shape=[jax.ShapeDtypeStruct(imag...]
  transfers between devices with their start and end apart: 8 -> 9, of which waited for: 4 -> 5; matrix products, arithmetic and copies ran while one was open for 0% -> 0% of each run, Pallas kernels for 0% -> 1%
where the time goes in v2:
time: 159 us
  blocking collectives  75.8 us (48%)
  Pallas kernels  36.3 us (23%)
  waiting for transfers between devices  24.9 us (16%)
  starting transfers between devices  19.2 us (12%)
  local copies, waits for them, and re-layouts  2.13 us (1%)
    all_to_all x2, blocking collectives, on_device(): lax.all_to_all(blend.reshape(cells, 1, share, half), ('row', 'col'), 0, 1...  47.5 us
    all_to_all x1, blocking collectives, on_device(): lax.all_to_all(gv.reshape(1, cells, share, half), ('row', 'col'), 1, 0, t...  28.3 us
    pallas_call x2, Pallas kernels, front(): pl.pallas_call(functools.partial(front_kernel, layer), out_shape=outs, in...  27.7 us
    all_to_all x1, waiting for transfers between devices, on_device(): lax.all_to_all(gv.reshape(1, cells, share, half), ('row', 'col'), 1, 0, t...  20.1 us
    all_to_all x1, starting transfers between devices, on_device(): lax.all_to_all(gv.reshape(1, cells, share, half), ('row', 'col'), 1, 0, t...  9.49 us
    ppermute x4, starting transfers between devices, traded(): far = lax.ppermute(far, axis, outer)  5.73 us
    ppermute x4, starting transfers between devices, traded(): near = lax.ppermute(near, axis, inner)  4.02 us
    pallas_call x2, Pallas kernels, back(): pl.pallas_call(functools.partial(back_kernel, layer, last), out_shape=out...  3.56 us
  transfers between devices with their start and end apart: 9, of which 5 were waited for; matrix products, arithmetic and copies ran while one was open for 0% of the time, Pallas kernels for 1%

profile of v2, /device:TPU:1, one launch (start us, length us, event | category | flops | bytes accessed | tf_op | source)
XLA Modules:
  0.0 158.7 jit_solution(10153254221425770991)
XLA Ops:
  0.0 0.9 row_strips.1
  0.9 0.1 collective-permute-start
  1.0 2.7 %collective-permute-start.1 = (bf16[2,64,256]{2,1,0:T(8,128)(2,1)S(1)}, bf16[2,64,256]{2,1,0:T(8,128)(2,1)S(1)}, u32[]{:S(2)}, u32[]{:S(2)}) collective-permute-start(bf16[2,64,256]{2,1,0:T(8,128)(2,1)S(1)} %get-tuple-element.37), channel_id=1, source_target_pairs={{4,8},{12,16},{20,24},{28,0},{8,4},{16,12},{24,20},{0,28},{5,9},{1... | collective-permute-start | bytes 196616 | tf_op jit(solution)/shard_map/ppermute | solution.py:561
  3.6 1.5 column_strips.1
  5.2 0.0 collective-permute-done.near_rows
  5.2 0.7 collective-permute-done.1.far_rows
  5.9 2.2 %collective-permute-start.2 = (bf16[2,52,256]{2,1,0:T(8,128)(2,1)S(1)}, bf16[2,52,256]{2,1,0:T(8,128)(2,1)S(1)}, u32[]{:S(2)}, u32[]{:S(2)}) collective-permute-start(bf16[2,52,256]{2,1,0:T(8,128)(2,1)S(1)} %get-tuple-element.40), channel_id=1, source_target_pairs={{0,1},{1,0},{2,3},{3,2},{4,5},{5,4},{6,7},{7,6},{8,9},{9,8},{10,11... | collective-permute-start | bytes 159752 | tf_op jit(solution)/shard_map/ppermute | solution.py:562
  8.2 0.7 collective-permute-start.3
  8.9 0.9 collective-permute-done.2.near_cols
  9.8 0.0 collective-permute-done.3.far_cols
  9.8 0.0 copy-start.2
  9.8 0.0 copy-start.7
  9.8 14.3 %front.2 = (f32[3072,256]{1,0:T(8,128)S(1)}, bf16[3072,128]{1,0:T(8,128)(2,1)S(1)}, bf16[3072,128]{1,0:T(8,128)(2,1)S(1)}, bf16[3072,128]{1,0:T(8,128)(2,1)S(1)}, bf16[3072,128]{1,0:T(8,128)(2,1)}) custom-call(bf16[48,64,256]{2,1,0:T(8,128)(2,1)S(1)} %get-tuple-element.35.cur_ref, bf16[2,64,256]{2,1,0:T(8,128)(2,1)S(1)} %collective-permute-done.near_rows, ...), custom_call_target="tpu_custom_call" | custom-call | flops 8053063680 | bytes 12582912 | tf_op jit(solution)/shard_map/front/pallas_call | solution.py:262
  24.1 0.0 copy-start
  24.1 1.6 %copy-done = f32[3072,256]{1,0:T(8,128)} copy-done((f32[3072,256]{1,0:T(8,128)}, f32[3072,256]{1,0:T(8,128)S(1)}, u32[]{:S(2)}) %copy-start) | copy-done | bytes 3145752
  25.7 0.0 copy-start.4
  25.7 0.0 copy-start.6
  25.7 0.0 copy-start.8
  25.7 0.0 copy-done.2
  25.7 0.0 copy-done.7
  25.7 0.4 local.2
  26.1 0.5 copy-done.4
  26.6 9.5 %all-to-all-start = ((bf16[1,32,96,128]{3,2,0,1:T(8,128)(2,1)}), bf16[1,32,96,128]{3,2,0,1:T(8,128)(2,1)S(1)}, u32[]{:S(2)}, u32[]{:S(2)}) async-start(bf16[1,32,96,128]{3,2,0,1:T(8,128)(2,1)} %bitcast.6), calls=%async_computation | async-start | bytes 1572864 | tf_op jit(solution)/shard_map/all_to_all | solution.py:657
  36.1 0.0 copy-done.6
  36.1 0.0 copy-done.8
  36.1 0.7 mixing_tiles.1
  36.8 20.1 %all-to-all-done = bf16[1,32,96,128]{3,2,0,1:T(8,128)(2,1)S(1)} async-done(((bf16[1,32,96,128]{3,2,0,1:T(8,128)(2,1)}), bf16[1,32,96,128]{3,2,0,1:T(8,128)(2,1)S(1)}, u32[]{:S(2)}, u32[]{:S(2)}) %all-to-all-start) | async-done | bytes 786464 | tf_op jit(solution)/shard_map/all_to_all | solution.py:657
  56.9 0.0 copy-start.1
  56.9 0.0 copy-start.3
  56.9 0.0 copy-start.5
  56.9 0.6 grid_mixing.2
  57.5 23.8 %all_to_all.16 = bf16[32,1,96,128]{3,2,1,0:T(8,128)(2,1)S(1)} all-to-all(bf16[32,1,96,128]{3,2,1,0:T(8,128)(2,1)S(1)} %bitcast.29), channel_id=1, replica_groups=mesh['row'=8,'col'=4] {'row','col'}, dimensions={0} | all-to-all | bytes 1572864 | tf_op jit(solution)/shard_map/all_to_all | solution.py:659
  81.2 0.0 copy-done.1
  81.2 0.0 copy-done.3
  81.2 0.0 copy-done.5
  81.2 1.5 back.2
  82.7 0.1 collective-permute-start.4
  82.8 1.6 %collective-permute-start.5 = (bf16[2,64,256]{2,1,0:T(8,128)(2,1)S(1)}, bf16[2,64,256]{2,1,0:T(8,128)(2,1)S(1)}, u32[]{:S(2)}, u32[]{:S(2)}) collective-permute-start(bf16[2,64,256]{2,1,0:T(8,128)(2,1)S(1)} %get-tuple-element.53), channel_id=1, source_target_pairs={{4,8},{12,16},{20,24},{28,0},{8,4},{16,12},{24,20},{0,28},{5,9},{1... | collective-permute-start | bytes 196616 | tf_op jit(solution)/shard_map/ppermute | solution.py:561
  84.4 0.0 collective-permute-done.4.near_rows
  84.4 2.5 %collective-permute-done.5.far_rows = bf16[2,64,256]{2,1,0:T(8,128)(2,1)S(1)} collective-permute-done((bf16[2,64,256]{2,1,0:T(8,128)(2,1)S(1)}, bf16[2,64,256]{2,1,0:T(8,128)(2,1)S(1)}, u32[]{:S(2)}, u32[]{:S(2)}) %collective-permute-start.5) | collective-permute-done | bytes 65568 | tf_op jit(solution)/shard_map/ppermute | solution.py:561
  86.9 1.6 %collective-permute-start.6 = (bf16[2,52,256]{2,1,0:T(8,128)(2,1)S(1)}, bf16[2,52,256]{2,1,0:T(8,128)(2,1)S(1)}, u32[]{:S(2)}, u32[]{:S(2)}) collective-permute-start(bf16[2,52,256]{2,1,0:T(8,128)(2,1)S(1)} %get-tuple-element.56), channel_id=1, source_target_pairs={{0,1},{1,0},{2,3},{3,2},{4,5},{5,4},{6,7},{7,6},{8,9},{9,8},{10,11... | collective-permute-start | bytes 159752 | tf_op jit(solution)/shard_map/ppermute | solution.py:562
  88.6 0.8 collective-permute-start.7
  89.4 0.7 collective-permute-done.6.near_cols
  90.1 0.0 collective-permute-done.7.far_cols
  90.1 13.4 %front.3 = (f32[3072,256]{1,0:T(8,128)S(1)}, bf16[3072,128]{1,0:T(8,128)(2,1)S(1)}, bf16[3072,128]{1,0:T(8,128)(2,1)S(1)}, bf16[3072,128]{1,0:T(8,128)(2,1)S(1)}, bf16[3072,128]{1,0:T(8,128)(2,1)S(1)}) custom-call(bf16[48,64,256]{2,1,0:T(8,128)(2,1)S(1)} %get-tuple-element.51.cur_ref, bf16[2,64,256]{2,1,0:T(8,128)(2,1)S(1)} %collective-permute-done.4.near_rows, ...), custom_call_target="tpu_custom_call" | custom-call | flops 8053063680 | bytes 12582912 | tf_op jit(solution)/shard_map/front/pallas_call | solution.py:262
  103.5 0.4 local.3
  103.9 28.3 %all_to_all.17 = bf16[1,32,96,128]{3,2,0,1:T(8,128)(2,1)S(1)} all-to-all(bf16[1,32,96,128]{3,2,0,1:T(8,128)(2,1)S(1)} %bitcast.32), channel_id=1, replica_groups=mesh['row'=8,'col'=4] {'row','col'}, dimensions={1} | all-to-all | bytes 1572864 | tf_op jit(solution)/shard_map/all_to_all | solution.py:657
  132.1 0.6 grid_mixing.3
  132.7 23.8 %all_to_all.18 = bf16[32,1,96,128]{3,2,1,0:T(8,128)(2,1)S(1)} all-to-all(bf16[32,1,96,128]{3,2,1,0:T(8,128)(2,1)S(1)} %bitcast.28), channel_id=1, replica_groups=mesh['row'=8,'col'=4] {'row','col'}, dimensions={0} | all-to-all | bytes 1572864 | tf_op jit(solution)/shard_map/all_to_all | solution.py:659
  156.5 2.1 %back.3 = bf16[48,64,256]{2,1,0:T(8,128)(2,1)} custom-call(f32[3072,256]{1,0:T(8,128)S(1)} %get-tuple-element.58.mixed_ref, bf16[3072,128]{1,0:T(8,128)(2,1)S(1)} %bitcast.25, bf16[3072,128]{1,0:T(8,128)(2,1)S(1)} %get-tuple-element.63.gu_ref, bf16[3072,128]{1,0:T(8,128)(2,1)S(1)} %bitcast.24, bf16[2,256,256]{2,1,0:T(8,128)(2,1)S(1)} %copy-done.3), custom_call_target="tpu_custom_call" | custom-call | flops 402653184 | bytes 7077888 | tf_op jit(solution)/shard_map/back/pallas_call | solution.py:478
  (2 shorter events, 0.1 us)
Async XLA Ops:
  0.9 4.3 %collective-permute-start = (bf16[2,64,256]{2,1,0:T(8,128)(2,1)S(1)}, bf16[2,64,256]{2,1,0:T(8,128)(2,1)S(1)}, u32[]{:S(2)}, u32[]{:S(2)}) collective-permute-start(bf16[2,64,256]{2,1,0:T(8,128)(2,1)S(1)} %get-tuple-element.36), channel_id=1, source_target_pairs={{0,4},{4,0},{8,12},{12,8},{16,20},{20,16},{24,28},{28,24},{1,5},{5... | collective-permute-start | bytes 196616 | tf_op jit(solution)/shard_map/ppermute | solution.py:562
  1.0 4.9 %collective-permute-start.1 = (bf16[2,64,256]{2,1,0:T(8,128)(2,1)S(1)}, bf16[2,64,256]{2,1,0:T(8,128)(2,1)S(1)}, u32[]{:S(2)}, u32[]{:S(2)}) collective-permute-start(bf16[2,64,256]{2,1,0:T(8,128)(2,1)S(1)} %get-tuple-element.37), channel_id=1, source_target_pairs={{4,8},{12,16},{20,24},{28,0},{8,4},{16,12},{24,20},{0,28},{5,9},{1... | collective-permute-start | bytes 196616 | tf_op jit(solution)/shard_map/ppermute | solution.py:561
  5.9 3.8 %collective-permute-start.2 = (bf16[2,52,256]{2,1,0:T(8,128)(2,1)S(1)}, bf16[2,52,256]{2,1,0:T(8,128)(2,1)S(1)}, u32[]{:S(2)}, u32[]{:S(2)}) collective-permute-start(bf16[2,52,256]{2,1,0:T(8,128)(2,1)S(1)} %get-tuple-element.40), channel_id=1, source_target_pairs={{0,1},{1,0},{2,3},{3,2},{4,5},{5,4},{6,7},{7,6},{8,9},{9,8},{10,11... | collective-permute-start | bytes 159752 | tf_op jit(solution)/shard_map/ppermute | solution.py:562
  8.2 1.6 collective-permute-start.3
  9.8 16.0 %copy-start.2 = (bf16[2,256,256]{2,1,0:T(8,128)(2,1)S(1)}, bf16[2,256,256]{2,1,0:T(8,128)(2,1)}, u32[]{:S(2)}) copy-start(bf16[2,256,256]{2,1,0:T(8,128)(2,1)} %mix_ref.3) | copy-start | bytes 786436
  9.8 16.0 %copy-start.7 = (f32[2,256]{1,0:T(2,128)S(1)}, f32[2,256]{1,0:T(2,128)}, u32[]{:S(2)}) copy-start(f32[2,256]{1,0:T(2,128)} %bias_ref.3) | copy-start | bytes 6148
  24.1 1.6 %copy-start = (f32[3072,256]{1,0:T(8,128)}, f32[3072,256]{1,0:T(8,128)S(1)}, u32[]{:S(2)}) copy-start(f32[3072,256]{1,0:T(8,128)S(1)} %get-tuple-element.42.mixed_ref) | copy-start | bytes 9437188
  25.7 0.9 copy-start.4
  25.7 10.4 %copy-start.6 = (bf16[2,32,32]{2,1,0:T(8,128)(2,1)S(1)}, bf16[2,32,32]{2,1,0:T(8,128)(2,1)}, u32[]{:S(2)}) copy-start(bf16[2,32,32]{2,1,0:T(8,128)(2,1)} %grid_ref.1) | copy-start | bytes 12292
  25.7 10.4 %copy-start.8 = (f32[2,32]{1,0:T(2,128)S(1)}, f32[2,32]{1,0:T(2,128)}, u32[]{:S(2)}) copy-start(f32[2,32]{1,0:T(2,128)} %grid_bias_ref.1) | copy-start | bytes 772
  26.6 30.3 %all-to-all-start = ((bf16[1,32,96,128]{3,2,0,1:T(8,128)(2,1)}), bf16[1,32,96,128]{3,2,0,1:T(8,128)(2,1)S(1)}, u32[]{:S(2)}, u32[]{:S(2)}) async-start(bf16[1,32,96,128]{3,2,0,1:T(8,128)(2,1)} %bitcast.6), calls=%async_computation | async-start | bytes 1572864 | tf_op jit(solution)/shard_map/all_to_all | solution.py:657
  56.9 24.3 %copy-start.1 = (f32[3072,256]{1,0:T(8,128)S(1)}, f32[3072,256]{1,0:T(8,128)}, u32[]{:S(2)}) copy-start(f32[3072,256]{1,0:T(8,128)} %copy-done) | copy-start | bytes 9437188
  56.9 24.3 %copy-start.3 = (bf16[2,256,256]{2,1,0:T(8,128)(2,1)S(1)}, bf16[2,256,256]{2,1,0:T(8,128)(2,1)}, u32[]{:S(2)}) copy-start(bf16[2,256,256]{2,1,0:T(8,128)(2,1)} %proj_ref.3) | copy-start | bytes 786436
  56.9 24.3 %copy-start.5 = (bf16[3072,128]{1,0:T(8,128)(2,1)S(1)}, bf16[3072,128]{1,0:T(8,128)(2,1)}, u32[]{:S(2)}) copy-start(bf16[3072,128]{1,0:T(8,128)(2,1)} %copy-done.4) | copy-start | bytes 2359300
  82.7 1.7 %collective-permute-start.4 = (bf16[2,64,256]{2,1,0:T(8,128)(2,1)S(1)}, bf16[2,64,256]{2,1,0:T(8,128)(2,1)S(1)}, u32[]{:S(2)}, u32[]{:S(2)}) collective-permute-start(bf16[2,64,256]{2,1,0:T(8,128)(2,1)S(1)} %get-tuple-element.52), channel_id=1, source_target_pairs={{0,4},{4,0},{8,12},{12,8},{16,20},{20,16},{24,28},{28,24},{1,5},{5... | collective-permute-start | bytes 196616 | tf_op jit(solution)/shard_map/ppermute | solution.py:562
  82.8 4.1 %collective-permute-start.5 = (bf16[2,64,256]{2,1,0:T(8,128)(2,1)S(1)}, bf16[2,64,256]{2,1,0:T(8,128)(2,1)S(1)}, u32[]{:S(2)}, u32[]{:S(2)}) collective-permute-start(bf16[2,64,256]{2,1,0:T(8,128)(2,1)S(1)} %get-tuple-element.53), channel_id=1, source_target_pairs={{4,8},{12,16},{20,24},{28,0},{8,4},{16,12},{24,20},{0,28},{5,9},{1... | collective-permute-start | bytes 196616 | tf_op jit(solution)/shard_map/ppermute | solution.py:561
  86.9 3.2 %collective-permute-start.6 = (bf16[2,52,256]{2,1,0:T(8,128)(2,1)S(1)}, bf16[2,52,256]{2,1,0:T(8,128)(2,1)S(1)}, u32[]{:S(2)}, u32[]{:S(2)}) collective-permute-start(bf16[2,52,256]{2,1,0:T(8,128)(2,1)S(1)} %get-tuple-element.56), channel_id=1, source_target_pairs={{0,1},{1,0},{2,3},{3,2},{4,5},{5,4},{6,7},{7,6},{8,9},{9,8},{10,11... | collective-permute-start | bytes 159752 | tf_op jit(solution)/shard_map/ppermute | solution.py:562
  88.6 1.6 collective-permute-start.7

commit v3 on v2

--- a/solution.py
+++ b/solution.py
@@ -455,8 +455,32 @@
         pltpu.make_async_copy(cur_ref, out_hbm, refs[1].at[0]).wait()
     else:
         *strip_refs, strip_ref = refs
-        keep_rows(cur_ref[0:RIM], cur_ref[rows - RIM : rows], *strip_refs[:2])
-        keep_columns(strip_ref, *strip_refs[2:])
+        keep_columns(strip_ref, *strip_refs)
+
+
+def ends_kernel(layer, mixed_ref, gl_ref, gu_ref, gm_ref, proj_ref, near_ref, far_ref):
+    pixels = mixed_ref.shape[0]
+    wide = near_ref.shape[0] * near_ref.shape[1]
+    found = []
+    for where in (slice(0, wide), slice(pixels - wide, pixels)):
+        gated = gu_ref[where].astype(jnp.float32) * gm_ref[where].astype(jnp.float32)
+        joined = jnp.concatenate([gl_ref[where], gated.astype(jnp.bfloat16)], axis=1)
+        total = mixed_ref[where] + jnp.dot(
+            joined, proj_ref[layer], preferred_element_type=jnp.float32
+        )
+        found.append(total.reshape(near_ref.shape).astype(jnp.bfloat16))
+    keep_rows(*found, near_ref, far_ref)
+
+
+def row_ends(layer, mixed, gl, gu, gm, proj, shape):
+    return pl.pallas_call(
+        functools.partial(ends_kernel, layer),
+        out_shape=strip_shapes(shape)[:2],
+        in_specs=[VMEM] * 5,
+        out_specs=[VMEM] * 2,
+        compiler_params=pltpu.CompilerParams(vmem_limit_bytes=16 * MIB),
+        name="row_ends",
+    )(mixed, gl, gu, gm, proj)
 
 
 def strip_shapes(shape):
@@ -473,7 +497,7 @@
     if last:
         scratch = [pltpu.VMEM(shape, jnp.bfloat16), pltpu.SemaphoreType.DMA((1,))]
     else:
-        outs += strip_shapes(shape)
+        outs += strip_shapes(shape)[2:]
         scratch = [pltpu.VMEM((2, RIM, rows, channels), f32)]
     return pl.pallas_call(
         functools.partial(back_kernel, layer, last),
@@ -657,16 +681,14 @@
         got = lax.all_to_all(gv.reshape(1, cells, share, half), ("row", "col"), 1, 0, tiled=True)
         blend = grid_mixing(layer, got.reshape(cells, share, half), mix_tiles, bias_tiles)
         gm = lax.all_to_all(blend.reshape(cells, 1, share, half), ("row", "col"), 0, 1, tiled=True)
-        current, *own = back(
-            layer,
-            last,
-            mixed,
-            gl.reshape(pixels, half),
-            gu,
-            gm.reshape(pixels, half),
-            proj_out,
-            image.shape,
-        )
+        parts = (mixed, gl.reshape(pixels, half), gu, gm.reshape(pixels, half), proj_out)
+        if last:
+            (current,) = back(layer, last, *parts, image.shape)
+        else:
+            rows_own = row_ends(layer, *parts, image.shape)
+        if not last:
+            current, *cols_own = back(layer, last, *parts, image.shape)
+            own = (*rows_own, *cols_own)
     return current
 
 

time: 159 us -> 160 us (level)
  local copies, waits for them, and re-layouts: 2.13 us -> 5.46 us
  waiting for transfers between devices: 24.9 us -> 21.7 us
    unnamed x18 -> x32, local copies, waits for them, and re-layouts: 2.13 us -> 5.46 us
    all_to_all x1, waiting for transfers between devices: 20.1 us -> 18.4 us  [on_device(): lax.all_to_all(gv.reshape(1, cells, share, half), ('row', 'col'), 1, 0, t...]
  transfers between devices with their start and end apart: 9 -> 9, of which waited for: 5 -> 5; matrix products, arithmetic and copies ran while one was open for 0% -> 0% of each run, Pallas kernels for 1% -> 2%
where the time goes in v3:
time: 160 us
  blocking collectives  75.8 us (47%)
  Pallas kernels  36.9 us (23%)
  waiting for transfers between devices  21.7 us (14%)
  starting transfers between devices  19.3 us (12%)
  local copies, waits for them, and re-layouts  5.46 us (3%)
    all_to_all x2, blocking collectives, on_device(): lax.all_to_all(blend.reshape(cells, 1, share, half), ('row', 'col'), 0, 1...  47.5 us
    all_to_all x1, blocking collectives, on_device(): lax.all_to_all(gv.reshape(1, cells, share, half), ('row', 'col'), 1, 0, t...  28.3 us
    pallas_call x2, Pallas kernels, front(): pl.pallas_call(functools.partial(front_kernel, layer), out_shape=outs, in...  26.8 us
    all_to_all x1, waiting for transfers between devices, on_device(): lax.all_to_all(gv.reshape(1, cells, share, half), ('row', 'col'), 1, 0, t...  18.4 us
    all_to_all x1, starting transfers between devices, on_device(): lax.all_to_all(gv.reshape(1, cells, share, half), ('row', 'col'), 1, 0, t...  9.54 us
    ppermute x4, starting transfers between devices, traded(): far = lax.ppermute(far, axis, outer)  5.72 us
    unnamed x32, local copies, waits for them, and re-layouts  5.46 us
    ppermute x4, starting transfers between devices, traded(): near = lax.ppermute(near, axis, inner)  4.02 us
  transfers between devices with their start and end apart: 9, of which 5 were waited for; matrix products, arithmetic and copies ran while one was open for 0% of the time, Pallas kernels for 2%

profile of v3, /device:TPU:1, one launch (start us, length us, event | category | flops | bytes accessed | tf_op | source)
XLA Modules:
  0.0 159.5 jit_solution(11831236660304924983)
XLA Ops:
  0.0 0.9 row_strips.1
  0.9 0.1 collective-permute-start
  1.0 2.7 %collective-permute-start.1 = (bf16[2,64,256]{2,1,0:T(8,128)(2,1)S(1)}, bf16[2,64,256]{2,1,0:T(8,128)(2,1)S(1)}, u32[]{:S(2)}, u32[]{:S(2)}) collective-permute-start(bf16[2,64,256]{2,1,0:T(8,128)(2,1)S(1)} %get-tuple-element.37), channel_id=1, source_target_pairs={{4,8},{12,16},{20,24},{28,0},{8,4},{16,12},{24,20},{0,28},{5,9},{1... | collective-permute-start | bytes 196616 | tf_op jit(solution)/shard_map/ppermute | solution.py:585
  3.6 1.5 column_strips.1
  5.2 0.0 collective-permute-done.near_rows
  5.2 0.7 collective-permute-done.1.far_rows
  5.9 2.2 %collective-permute-start.2 = (bf16[2,52,256]{2,1,0:T(8,128)(2,1)S(1)}, bf16[2,52,256]{2,1,0:T(8,128)(2,1)S(1)}, u32[]{:S(2)}, u32[]{:S(2)}) collective-permute-start(bf16[2,52,256]{2,1,0:T(8,128)(2,1)S(1)} %get-tuple-element.40), channel_id=1, source_target_pairs={{0,1},{1,0},{2,3},{3,2},{4,5},{5,4},{6,7},{7,6},{8,9},{9,8},{10,11... | collective-permute-start | bytes 159752 | tf_op jit(solution)/shard_map/ppermute | solution.py:586
  8.2 0.7 collective-permute-start.3
  8.9 0.9 collective-permute-done.2.near_cols
  9.8 0.0 collective-permute-done.3.far_cols
  9.8 0.0 copy-start.11
  9.8 0.0 copy-start.14
  9.8 13.4 %front.2 = (f32[3072,256]{1,0:T(8,128)S(1)}, bf16[3072,128]{1,0:T(8,128)(2,1)S(1)}, bf16[3072,128]{1,0:T(8,128)(2,1)S(1)}, bf16[3072,128]{1,0:T(8,128)(2,1)S(1)}, bf16[3072,128]{1,0:T(8,128)(2,1)S(1)}) custom-call(bf16[48,64,256]{2,1,0:T(8,128)(2,1)S(1)} %get-tuple-element.35.cur_ref, bf16[2,64,256]{2,1,0:T(8,128)(2,1)S(1)} %collective-permute-done.near_rows, ...), custom_call_target="tpu_custom_call" | custom-call | flops 8053063680 | bytes 12582912 | tf_op jit(solution)/shard_map/front/pallas_call | solution.py:262
  23.2 0.0 copy-start.5
  23.2 0.0 copy-start.12
  23.2 0.0 copy-start.13
  23.2 0.0 copy-start.15
  23.2 0.0 copy-done.11
  23.2 0.0 copy-done.14
  23.3 0.4 local.2
  23.6 0.5 copy-done.5
  24.1 0.0 copy-start
  24.1 0.9 copy-done
  25.0 0.0 copy-done.12
  25.0 9.5 %all-to-all-start = ((bf16[1,32,96,128]{3,2,0,1:T(8,128)(2,1)}), bf16[1,32,96,128]{3,2,0,1:T(8,128)(2,1)}, u32[]{:S(2)}, u32[]{:S(2)}) async-start(bf16[1,32,96,128]{3,2,0,1:T(8,128)(2,1)} %bitcast.33), calls=%async_computation | async-start | bytes 1572864 | tf_op jit(solution)/shard_map/all_to_all | solution.py:681
  34.6 0.0 copy-done.13
  34.6 0.0 copy-done.15
  34.6 0.7 mixing_tiles.1
  35.3 0.0 copy-start.2
  35.3 1.0 copy-done.2
  36.3 0.0 copy-start.8
  36.3 0.8 copy-done.8
  37.1 18.4 %all-to-all-done = bf16[1,32,96,128]{3,2,0,1:T(8,128)(2,1)} async-done(((bf16[1,32,96,128]{3,2,0,1:T(8,128)(2,1)}), bf16[1,32,96,128]{3,2,0,1:T(8,128)(2,1)}, u32[]{:S(2)}, u32[]{:S(2)}) %all-to-all-start) | async-done | bytes 786464 | tf_op jit(solution)/shard_map/all_to_all | solution.py:681
  55.4 0.0 copy-start.3
  55.4 1.2 copy-done.3
  56.7 0.0 copy-start.9
  56.7 1.0 copy-done.9
  57.7 0.0 copy-start.1
  57.7 0.0 copy-start.6
  57.7 1.8 %grid_mixing.2 = bf16[32,96,128]{2,1,0:T(8,128)(2,1)S(1)} custom-call(bf16[32,96,128]{2,1,0:T(8,128)(2,1)} %bitcast.7.got_ref, bf16[2,512,512]{2,1,0:T(8,128)(2,1)S(1)} %copy-done.3, f32[2,512,128]{2,1,0:T(8,128)S(1)} %copy-done.9), custom_call_target="tpu_custom_call" | custom-call | tf_op jit(solution)/shard_map/grid_mixing/pallas_call | solution.py:395
  59.5 23.8 %all_to_all.16 = bf16[32,1,96,128]{3,2,1,0:T(8,128)(2,1)S(1)} all-to-all(bf16[32,1,96,128]{3,2,1,0:T(8,128)(2,1)S(1)} %bitcast.32), channel_id=1, replica_groups=mesh['row'=8,'col'=4] {'row','col'}, dimensions={0} | all-to-all | bytes 1572864 | tf_op jit(solution)/shard_map/all_to_all | solution.py:683
  83.3 0.0 copy-done.1
  83.3 0.0 copy-done.6
  83.3 0.0 copy-done.7
  83.3 0.2 row_ends.1
  83.5 0.1 collective-permute-start.4
  83.6 1.6 collective-permute-start.5
  85.2 1.5 back.2
  86.7 0.0 collective-permute-done.4.near_rows
  86.7 1.0 collective-permute-done.5.far_rows
  87.7 1.6 %collective-permute-start.6 = (bf16[2,52,256]{2,1,0:T(8,128)(2,1)S(1)}, bf16[2,52,256]{2,1,0:T(8,128)(2,1)S(1)}, u32[]{:S(2)}, u32[]{:S(2)}) collective-permute-start(bf16[2,52,256]{2,1,0:T(8,128)(2,1)S(1)} %get-tuple-element.56), channel_id=1, source_target_pairs={{0,1},{1,0},{2,3},{3,2},{4,5},{5,4},{6,7},{7,6},{8,9},{9,8},{10,11... | collective-permute-start | bytes 159752 | tf_op jit(solution)/shard_map/ppermute | solution.py:586
  89.4 0.8 collective-permute-start.7
  90.2 0.7 collective-permute-done.6.near_cols
  90.9 0.0 collective-permute-done.7.far_cols
  90.9 13.4 %front.3 = (f32[3072,256]{1,0:T(8,128)S(1)}, bf16[3072,128]{1,0:T(8,128)(2,1)S(1)}, bf16[3072,128]{1,0:T(8,128)(2,1)S(1)}, bf16[3072,128]{1,0:T(8,128)(2,1)S(1)}, bf16[3072,128]{1,0:T(8,128)(2,1)S(1)}) custom-call(bf16[48,64,256]{2,1,0:T(8,128)(2,1)S(1)} %get-tuple-element.51.cur_ref, bf16[2,64,256]{2,1,0:T(8,128)(2,1)S(1)} %collective-permute-done.4.near_rows, ...), custom_call_target="tpu_custom_call" | custom-call | flops 8053063680 | bytes 12582912 | tf_op jit(solution)/shard_map/front/pallas_call | solution.py:262
  104.3 0.0 copy-start.4
  104.3 0.0 copy-start.10
  104.3 0.4 local.3
  104.7 28.3 %all_to_all.17 = bf16[1,32,96,128]{3,2,0,1:T(8,128)(2,1)S(1)} all-to-all(bf16[1,32,96,128]{3,2,0,1:T(8,128)(2,1)S(1)} %bitcast.34), channel_id=1, replica_groups=mesh['row'=8,'col'=4] {'row','col'}, dimensions={1} | all-to-all | bytes 1572864 | tf_op jit(solution)/shard_map/all_to_all | solution.py:681
  133.0 0.0 copy-done.4
  133.0 0.0 copy-done.10
  133.0 0.6 grid_mixing.3
  133.5 23.8 %all_to_all.18 = bf16[32,1,96,128]{3,2,1,0:T(8,128)(2,1)S(1)} all-to-all(bf16[32,1,96,128]{3,2,1,0:T(8,128)(2,1)S(1)} %bitcast.31), channel_id=1, replica_groups=mesh['row'=8,'col'=4] {'row','col'}, dimensions={0} | all-to-all | bytes 1572864 | tf_op jit(solution)/shard_map/all_to_all | solution.py:683
  157.3 2.1 %back.3 = bf16[48,64,256]{2,1,0:T(8,128)(2,1)} custom-call(f32[3072,256]{1,0:T(8,128)S(1)} %get-tuple-element.58.mixed_ref, bf16[3072,128]{1,0:T(8,128)(2,1)S(1)} %bitcast.29, bf16[3072,128]{1,0:T(8,128)(2,1)S(1)} %get-tuple-element.63.gu_ref, bf16[3072,128]{1,0:T(8,128)(2,1)S(1)} %bitcast.28, bf16[2,256,256]{2,1,0:T(8,128)(2,1)S(1)} %copy-done.7), custom_call_target="tpu_custom_call" | custom-call | flops 402653184 | bytes 7077888 | tf_op jit(solution)/shard_map/back/pallas_call | solution.py:502
  (3 shorter events, 0.1 us)
Async XLA Ops:
  0.9 4.3 %collective-permute-start = (bf16[2,64,256]{2,1,0:T(8,128)(2,1)S(1)}, bf16[2,64,256]{2,1,0:T(8,128)(2,1)S(1)}, u32[]{:S(2)}, u32[]{:S(2)}) collective-permute-start(bf16[2,64,256]{2,1,0:T(8,128)(2,1)S(1)} %get-tuple-element.36), channel_id=1, source_target_pairs={{0,4},{4,0},{8,12},{12,8},{16,20},{20,16},{24,28},{28,24},{1,5},{5... | collective-permute-start | bytes 196616 | tf_op jit(solution)/shard_map/ppermute | solution.py:586
  1.0 4.9 %collective-permute-start.1 = (bf16[2,64,256]{2,1,0:T(8,128)(2,1)S(1)}, bf16[2,64,256]{2,1,0:T(8,128)(2,1)S(1)}, u32[]{:S(2)}, u32[]{:S(2)}) collective-permute-start(bf16[2,64,256]{2,1,0:T(8,128)(2,1)S(1)} %get-tuple-element.37), channel_id=1, source_target_pairs={{4,8},{12,16},{20,24},{28,0},{8,4},{16,12},{24,20},{0,28},{5,9},{1... | collective-permute-start | bytes 196616 | tf_op jit(solution)/shard_map/ppermute | solution.py:585
  5.9 3.8 %collective-permute-start.2 = (bf16[2,52,256]{2,1,0:T(8,128)(2,1)S(1)}, bf16[2,52,256]{2,1,0:T(8,128)(2,1)S(1)}, u32[]{:S(2)}, u32[]{:S(2)}) collective-permute-start(bf16[2,52,256]{2,1,0:T(8,128)(2,1)S(1)} %get-tuple-element.40), channel_id=1, source_target_pairs={{0,1},{1,0},{2,3},{3,2},{4,5},{5,4},{6,7},{7,6},{8,9},{9,8},{10,11... | collective-permute-start | bytes 159752 | tf_op jit(solution)/shard_map/ppermute | solution.py:586
  8.2 1.6 collective-permute-start.3
  9.8 13.5 %copy-start.11 = (bf16[2,256,256]{2,1,0:T(8,128)(2,1)S(1)}, bf16[2,256,256]{2,1,0:T(8,128)(2,1)}, u32[]{:S(2)}) copy-start(bf16[2,256,256]{2,1,0:T(8,128)(2,1)} %mix_ref.3) | copy-start | bytes 786436
  9.8 13.5 %copy-start.14 = (f32[2,256]{1,0:T(2,128)S(1)}, f32[2,256]{1,0:T(2,128)}, u32[]{:S(2)}) copy-start(f32[2,256]{1,0:T(2,128)} %bias_ref.3) | copy-start | bytes 6148
  23.2 0.9 copy-start.5
  23.2 1.8 %copy-start.12 = (bf16[3072,128]{1,0:T(8,128)(2,1)}, bf16[3072,128]{1,0:T(8,128)(2,1)S(1)}, u32[]{:S(2)}) copy-start(bf16[3072,128]{1,0:T(8,128)(2,1)S(1)} %get-tuple-element.48) | copy-start | bytes 2359300
  23.2 11.4 %copy-start.13 = (bf16[2,32,32]{2,1,0:T(8,128)(2,1)S(1)}, bf16[2,32,32]{2,1,0:T(8,128)(2,1)}, u32[]{:S(2)}) copy-start(bf16[2,32,32]{2,1,0:T(8,128)(2,1)} %grid_ref.1) | copy-start | bytes 12292
  23.2 11.4 %copy-start.15 = (f32[2,32]{1,0:T(2,128)S(1)}, f32[2,32]{1,0:T(2,128)}, u32[]{:S(2)}) copy-start(f32[2,32]{1,0:T(2,128)} %grid_bias_ref.1) | copy-start | bytes 772
  24.1 0.9 copy-start
  25.0 30.4 %all-to-all-start = ((bf16[1,32,96,128]{3,2,0,1:T(8,128)(2,1)}), bf16[1,32,96,128]{3,2,0,1:T(8,128)(2,1)}, u32[]{:S(2)}, u32[]{:S(2)}) async-start(bf16[1,32,96,128]{3,2,0,1:T(8,128)(2,1)} %bitcast.33), calls=%async_computation | async-start | bytes 1572864 | tf_op jit(solution)/shard_map/all_to_all | solution.py:681
  35.3 1.0 copy-start.2
  36.3 0.8 copy-start.8
  55.4 1.2 copy-start.3
  56.7 1.0 copy-start.9
  57.7 25.6 %copy-start.1 = (bf16[48,64,128]{2,1,0:T(8,128)(2,1)S(1)}, bf16[48,64,128]{2,1,0:T(8,128)(2,1)}, u32[]{:S(2)}) copy-start(bf16[48,64,128]{2,1,0:T(8,128)(2,1)} %copy-done) | copy-start | bytes 2359300
  57.7 25.6 %copy-start.6 = (bf16[3072,128]{1,0:T(8,128)(2,1)S(1)}, bf16[3072,128]{1,0:T(8,128)(2,1)}, u32[]{:S(2)}) copy-start(bf16[3072,128]{1,0:T(8,128)(2,1)} %copy-done.5) | copy-start | bytes 2359300
  57.7 25.6 %copy-start.7 = (bf16[2,256,256]{2,1,0:T(8,128)(2,1)S(1)}, bf16[2,256,256]{2,1,0:T(8,128)(2,1)}, u32[]{:S(2)}) copy-start(bf16[2,256,256]{2,1,0:T(8,128)(2,1)} %proj_ref.5) | copy-start | bytes 786436
  83.5 3.1 %collective-permute-start.4 = (bf16[2,64,256]{2,1,0:T(8,128)(2,1)S(1)}, bf16[2,64,256]{2,1,0:T(8,128)(2,1)S(1)}, u32[]{:S(2)}, u32[]{:S(2)}) collective-permute-start(bf16[2,64,256]{2,1,0:T(8,128)(2,1)S(1)} %get-tuple-element.52), channel_id=1, source_target_pairs={{0,4},{4,0},{8,12},{12,8},{16,20},{20,16},{24,28},{28,24},{1,5},{5... | collective-permute-start | bytes 196616 | tf_op jit(solution)/shard_map/ppermute | solution.py:586
  83.6 4.1 %collective-permute-start.5 = (bf16[2,64,256]{2,1,0:T(8,128)(2,1)S(1)}, bf16[2,64,256]{2,1,0:T(8,128)(2,1)S(1)}, u32[]{:S(2)}, u32[]{:S(2)}) collective-permute-start(bf16[2,64,256]{2,1,0:T(8,128)(2,1)S(1)} %get-tuple-element.53), channel_id=1, source_target_pairs={{4,8},{12,16},{20,24},{28,0},{8,4},{16,12},{24,20},{0,28},{5,9},{1... | collective-permute-start | bytes 196616 | tf_op jit(solution)/shard_map/ppermute | solution.py:585
  87.7 3.2 %collective-permute-start.6 = (bf16[2,52,256]{2,1,0:T(8,128)(2,1)S(1)}, bf16[2,52,256]{2,1,0:T(8,128)(2,1)S(1)}, u32[]{:S(2)}, u32[]{:S(2)}) collective-permute-start(bf16[2,52,256]{2,1,0:T(8,128)(2,1)S(1)} %get-tuple-element.56), channel_id=1, source_target_pairs={{0,1},{1,0},{2,3},{3,2},{4,5},{5,4},{6,7},{7,6},{8,9},{9,8},{10,11... | collective-permute-start | bytes 159752 | tf_op jit(solution)/shard_map/ppermute | solution.py:586
  89.4 1.6 collective-permute-start.7
  104.3 28.7 %copy-start.4 = (bf16[2,512,512]{2,1,0:T(8,128)(2,1)S(1)}, bf16[2,512,512]{2,1,0:T(8,128)(2,1)}, u32[]{:S(2)}) copy-start(bf16[2,512,512]{2,1,0:T(8,128)(2,1)} %copy-done.2) | copy-start | bytes 3145732
  104.3 28.7 %copy-start.10 = (f32[2,512,128]{2,1,0:T(8,128)S(1)}, f32[2,512,128]{2,1,0:T(8,128)}, u32[]{:S(2)}) copy-start(f32[2,512,128]{2,1,0:T(8,128)} %copy-done.8) | copy-start | bytes 1572868
